TPU v7x, 32 devices: a whole 2x2x4 slice. The times are simulated.
32 devices in a mesh: groups: 2 (over x), blk: 16 (over z, y, core).
Axes of the slice: x: 2, y: 2, z: 4, core: 2. Of those that a mesh axis runs over, the one named last changes fastest.
Arguments:
- query: bfloat16 [8192, 1024], P(('groups', 'blk')), parts along dimension 0, may hold values from -5 to 5
- key_in: bfloat16 [8192, 1024], P(('groups', 'blk')), parts along dimension 0, may hold values from -6 to 6
- value: bfloat16 [8192, 1024], P(('groups', 'blk')), parts along dimension 0, may hold values from -6 to 6
- grad_out: bfloat16 [8192, 1024], P(('groups', 'blk')), parts along dimension 0, may hold values from -6 to 6
- neighbors: int32 [64, 8], P(('groups', 'blk')), parts along dimension 0, may hold values from 0 to 31, as said below
- counts: int32 [64], P(('groups', 'blk')), parts along dimension 0, may hold values from 2 to 8, as said below
Outputs:
- attn_out: bfloat16 [8192, 1024], P(('groups', 'blk')), parts along dimension 0
- grad_query: bfloat16 [8192, 1024], P(('groups', 'blk')), parts along dimension 0
- grad_key: bfloat16 [8192, 1024], P(('groups', 'blk')), parts along dimension 0
- grad_value: bfloat16 [8192, 1024], P(('groups', 'blk')), parts along dimension 0
There are 2 independent parts, one for each index of `groups`. A program takes and returns all parts, laid end to end along the dimension named above; each array names one. Nothing has to cross between parts.
Inputs may be any that keep to these rules, and one draw needn't show every extreme that they name: `neighbors`: row b holds 8 distinct block indices; its first entry is b itself; every entry is a block whose device (block // 2) is at most 2 steps from b's device along blk, counted cyclically; only the first counts[b] entries are used. `counts`: some block has exactly 8 and some exactly 2.
All inputs are finite; a program needn't handle non-finite values.
Results may differ from a plain program's by a relative error of at most 0.0086.
Values may be sent and summed in bfloat16 or wider, within the bound.
No kernel may reach another device: no remote copies, remote signals or barrier semaphores. Data moves between devices by JAX's collectives and lax.ppermute only.
A program may use at most 128 MiB of HBM per device.

v0:
```python
import math

import jax
import jax.numpy as jnp
from jax import lax
from jax.sharding import PartitionSpec as P

HEADS = 16
REACH = 2


def shifted(x, axis, by):
    length = lax.axis_size(axis)
    return lax.ppermute(x, axis, [(i, (i + by) % length) for i in range(length)])


def split_heads(matrix):
    return matrix.reshape(matrix.shape[0], HEADS, matrix.shape[1] // HEADS)


def merge_heads(matrix):
    return matrix.reshape(matrix.shape[0], matrix.shape[1] * matrix.shape[2])


def block_slice(matrix, blk_id, blk_len):
    return lax.dynamic_slice_in_dim(matrix, blk_id * blk_len, blk_len, 0)


def local(query, key_in, value, grad_out, neighbors, counts):
    row_count, model_width = query.shape
    own_blocks = neighbors.shape[0]
    list_width = neighbors.shape[1]
    blk_len = row_count // own_blocks
    head_dim = model_width // HEADS
    factor = 1.0 / math.sqrt(head_dim)
    shard_count = lax.axis_size("blk")
    shard_index = lax.axis_index("blk")
    span_blocks = (2 * REACH + 1) * own_blocks
    paired = jnp.stack([key_in, value])
    pieces = {0: paired}
    for direction in (1, -1):
        current = paired
        for distance in range(1, REACH + 1):
            current = shifted(current, "blk", -direction)
            pieces[direction * distance] = current
    window = jnp.concatenate([pieces[offset] for offset in range(-REACH, REACH + 1)], axis=1)
    window_tiles = window.reshape(2, span_blocks, blk_len, model_width)
    shard_pos = jnp.mod(neighbors // own_blocks - shard_index + REACH, shard_count)
    slot_table = shard_pos * own_blocks + neighbors % own_blocks
    slot_ids = jnp.arange(list_width, dtype=jnp.int32)

    def block_inputs(blk_id):
        slots = slot_table[blk_id]
        picked = window_tiles[:, slots]
        k_all = split_heads(picked[0].reshape(list_width * blk_len, model_width))
        v_all = split_heads(picked[1].reshape(list_width * blk_len, model_width))
        live_keys = jnp.repeat(slot_ids < counts[blk_id], blk_len)
        q_tile = split_heads(block_slice(query, blk_id, blk_len))
        scores = (
            jnp.einsum("qhd,khd->hqk", q_tile, k_all, preferred_element_type=jnp.float32) * factor
        )
        scores = jnp.where(live_keys[None, None, :], scores, -jnp.inf)
        return (slots, q_tile, k_all, v_all, scores)

    def forward_block(blk_id):
        slots, q_tile, k_all, v_all, scores = block_inputs(blk_id)
        row_top = jnp.max(scores, axis=2)
        exponent = jnp.exp(scores - row_top[:, :, None])
        row_sum = jnp.sum(exponent, axis=2)
        rounded = (exponent / row_sum[:, :, None]).astype(jnp.bfloat16)
        mixed = jnp.einsum("hqk,khd->qhd", rounded, v_all, preferred_element_type=jnp.float32)
        return (merge_heads(mixed).astype(jnp.bfloat16), row_top, row_sum)

    out_blocks, row_tops, row_sums = lax.map(forward_block, jnp.arange(own_blocks, dtype=jnp.int32))
    attn_out = out_blocks.reshape(row_count, model_width)
    row_delta = jnp.sum(
        split_heads(grad_out).astype(jnp.float32) * split_heads(attn_out).astype(jnp.float32),
        axis=2,
    )

    def query_pass(grad_window):

        def outer_step(grad_win, blk_id):
            slots, q_tile, k_all, v_all, scores = block_inputs(blk_id)
            g_tile = split_heads(block_slice(grad_out, blk_id, blk_len))
            delta_tile = block_slice(row_delta, blk_id, blk_len).T
            soft_probs = (
                jnp.exp(scores - row_tops[blk_id][:, :, None]) / row_sums[blk_id][:, :, None]
            )
            dprobs = jnp.einsum("qhd,khd->hqk", g_tile, v_all, preferred_element_type=jnp.float32)
            dscores = (soft_probs * (dprobs - delta_tile[:, :, None])).astype(jnp.bfloat16)
            grad_q = (
                jnp.einsum("hqk,khd->qhd", dscores, k_all, preferred_element_type=jnp.float32)
                * factor
            )
            probs_rounded = soft_probs.astype(jnp.bfloat16)
            dk_all = (
                jnp.einsum("hqk,qhd->khd", dscores, q_tile, preferred_element_type=jnp.float32)
                * factor
            )
            dv_all = jnp.einsum(
                "hqk,qhd->khd", probs_rounded, g_tile, preferred_element_type=jnp.float32
            )
            grad_win = grad_win.at[0, slots].add(dk_all.reshape(list_width, blk_len, model_width))
            grad_win = grad_win.at[1, slots].add(dv_all.reshape(list_width, blk_len, model_width))
            return (grad_win, merge_heads(grad_q))

        grad_win, grad_blocks = lax.scan(
            outer_step, grad_window, jnp.arange(own_blocks, dtype=jnp.int32)
        )
        return (grad_blocks.reshape(row_count, model_width), grad_win)

    grad_all, grad_tiles = query_pass(
        jnp.zeros((2, span_blocks, blk_len, model_width), jnp.float32)
    )
    grad_win = grad_tiles.reshape(2, span_blocks * blk_len, model_width)

    def window_piece(offset):
        return lax.slice_in_dim(
            grad_win, (offset + REACH) * row_count, (offset + REACH + 1) * row_count, axis=1
        )

    summed = window_piece(0)
    for direction in (1, -1):
        carried = window_piece(direction * REACH)
        for distance in range(REACH - 1, -1, -1):
            carried = shifted(carried.astype(jnp.bfloat16), "blk", direction).astype(carried.dtype)
            if distance > 0:
                carried = carried + window_piece(direction * distance)
        summed = summed + carried
    grad_key = summed[0].astype(jnp.bfloat16)
    grad_value = summed[1].astype(jnp.bfloat16)
    grad_query = grad_all.astype(jnp.bfloat16)
    return (attn_out, grad_query, grad_key, grad_value)


def solution(mesh):
    in_specs = (
        P(("groups", "blk"), None),
        P(("groups", "blk"), None),
        P(("groups", "blk"), None),
        P(("groups", "blk"), None),
        P(("groups", "blk"), None),
        P(("groups", "blk")),
    )
    out_specs = (
        P(("groups", "blk"), None),
        P(("groups", "blk"), None),
        P(("groups", "blk"), None),
        P(("groups", "blk"), None),
    )
    return jax.shard_map(local, mesh=mesh, in_specs=in_specs, out_specs=out_specs, check_vma=False)
```

profile of v0, /device:TPU:1, one launch (start us, length us, event | category | flops | bytes accessed | tf_op | source)
XLA Modules:
  0.0 352.5 jit_solution(11672745346984228568)
XLA Ops:
  2.0 2.7 collective-permute-start
  4.7 23.0 %collective-permute-done = bf16[2,256,1024]{2,1,0:T(8,128)(2,1)} collective-permute-done((bf16[2,256,1024]{2,1,0:T(8,128)(2,1)S(1)}, bf16[2,256,1024]{2,1,0:T(8,128)(2,1)}, u32[]{:S(2)}, u32[]{:S(2)}) %collective-permute-start) | collective-permute-done | bytes 1048608 | tf_op jit(solution)/shard_map/ppermute | solution.py:14
  27.7 2.6 collective-permute-start.1
  30.3 11.1 %collective-permute-done.2 = bf16[2,256,1024]{2,1,0:T(8,128)(2,1)S(1)} collective-permute-done((bf16[2,256,1024]{2,1,0:T(8,128)(2,1)S(1)}, bf16[2,256,1024]{2,1,0:T(8,128)(2,1)S(1)}, u32[]{:S(2)}, u32[]{:S(2)}) %collective-permute-start.2) | collective-permute-done | bytes 1048608 | tf_op jit(solution)/shard_map/ppermute | solution.py:14
  42.7 2.0 copy.32
  44.7 7.8 %collective-permute-done.1 = bf16[2,256,1024]{2,1,0:T(8,128)(2,1)} collective-permute-done((bf16[2,256,1024]{2,1,0:T(8,128)(2,1)}, bf16[2,256,1024]{2,1,0:T(8,128)(2,1)}, u32[]{:S(2)}, u32[]{:S(2)}) %collective-permute-start.1) | collective-permute-done | bytes 1048608 | tf_op jit(solution)/shard_map/ppermute | solution.py:14
  57.1 2.3 copy-done
  59.4 69.0 %while.28 = (s32[]{:T(128)}, bf16[2,128,1024]{1,2,0:T(8,128)(2,1)}, f32[2,16,128]{2,1,0:T(8,128)S(1)}, f32[2,16,128]{2,1,0:T(8,128)S(1)}, s32[2]{0:T(128)S(1)}, ...) while((s32[]{:T(128)}, bf16[2,128,1024]{1,2,0:T(8,128)(2,1)}, ...), condition=%wide.region_3.4_spmd.clone, body=%wide.region_0.3_spmd.clone.sunk | while | flops 562164736 | bytes 77152744 | solution.py:74
  64.3 5.3 %gather_fusion = bf16[8,2,128,1024]{3,2,1,0:T(8,128)(2,1)} fusion(bf16[2,10,128,1024]{3,2,1,0:T(8,128)(2,1)} %get-tuple-element.471, s32[1024]{0:T(1024)S(1)} %pad_clamp_fusion.4), kind=kCustom, calls=%fused_computation.clone.clone.1 | custom fusion | bytes 8388640 | tf_op jit(solution)/shard_map/while/body/eval_jaxpr/gather | solution.py:54
  69.6 4.8 %fusion.62 = (bf16[1,8,128,1024]{3,2,0,1:T(8,128)(2,1)}, bf16[1,8,128,1024]{3,2,0,1:T(8,128)(2,1)}) fusion(bf16[2,8,128,1024]{3,2,0,1:T(8,128)(2,1)} %bitcast.180), kind=kLoop, calls=%fused_computation.77.clone.1 | loop fusion | bytes 8388608 | tf_op jit(solution)/shard_map/while/body/eval_jaxpr/slice | solution.py:55
  74.4 3.4 copy.44
  77.8 2.3 squeeze.49
  80.1 4.2 %copy.45 = bf16[1,8,128,1024]{2,1,3,0:T(8,128)(2,1)} copy(bf16[1,8,128,1024]{3,2,0,1:T(8,128)(2,1)} %get-tuple-element.412) | data formatting | bytes 4194304 | tf_op jit(solution)/shard_map/while/body/eval_jaxpr/slice | solution.py:55
  84.2 2.8 squeeze.50
  88.5 2.0 fusion.64
  90.5 2.5 fusion.65
  98.8 5.3 %gather_fusion = bf16[8,2,128,1024]{3,2,1,0:T(8,128)(2,1)} fusion(bf16[2,10,128,1024]{3,2,1,0:T(8,128)(2,1)} %get-tuple-element.471, s32[1024]{0:T(1024)S(1)} %pad_clamp_fusion.4), kind=kCustom, calls=%fused_computation.clone.clone.1 | custom fusion | bytes 8388640 | tf_op jit(solution)/shard_map/while/body/eval_jaxpr/gather | solution.py:54
  104.1 4.8 %fusion.62 = (bf16[1,8,128,1024]{3,2,0,1:T(8,128)(2,1)}, bf16[1,8,128,1024]{3,2,0,1:T(8,128)(2,1)}) fusion(bf16[2,8,128,1024]{3,2,0,1:T(8,128)(2,1)} %bitcast.180), kind=kLoop, calls=%fused_computation.77.clone.1 | loop fusion | bytes 8388608 | tf_op jit(solution)/shard_map/while/body/eval_jaxpr/slice | solution.py:55
  108.9 3.4 copy.44
  112.3 2.3 squeeze.49
  114.6 4.2 %copy.45 = bf16[1,8,128,1024]{2,1,3,0:T(8,128)(2,1)} copy(bf16[1,8,128,1024]{3,2,0,1:T(8,128)(2,1)} %get-tuple-element.412) | data formatting | bytes 4194304 | tf_op jit(solution)/shard_map/while/body/eval_jaxpr/slice | solution.py:55
  118.7 2.8 squeeze.50
  123.0 2.0 fusion.64
  125.0 2.5 fusion.65
  128.4 1.6 copy.30
  132.1 5.3 %broadcast_in_dim.60 = f32[2,10,128,1024]{3,2,1,0:T(8,128)} broadcast(f32[]{:T(128)} %constant.94.clone.1), dimensions={} | broadcast | bytes 10485764 | tf_op jit(solution)/shard_map/broadcast_in_dim | solution.py:114
  137.4 153.3 %while.29 = (s32[]{:T(128)}, f32[2,10,128,1024]{3,2,1,0:T(8,128)}, bf16[2,128,1024]{1,2,0:T(8,128)(2,1)}, s32[2]{0:T(128)S(1)}, s32[2,8]{1,0:T(2,128)S(1)}, /*in...) while((s32[]{:T(128)}, f32[2,10,128,1024]{3,2,1,0:T(8,128)}, ...), condition=%wide.region_8.9_spmd.clone, body=%wide.region_5.8_spmd.clone.sunk | while | flops 1362363520 | bytes 160250608 | solution.py:108
  143.0 5.3 %gather_fusion.1 = bf16[8,2,128,1024]{3,2,1,0:T(8,128)(2,1)} fusion(bf16[2,10,128,1024]{3,2,1,0:T(8,128)(2,1)} %get-tuple-element.520, s32[1024]{0:T(1024)S(1)} %pad_clamp_fusion.5), kind=kCustom, calls=%fused_computation.1.clone.clone.1 | custom fusion | bytes 8388640 | tf_op jit(solution)/shard_map/while/body/eval_jaxpr/gather | solution.py:54
  148.2 4.2 %fusion.76 = (bf16[1,8,128,1024]{3,2,0,1:T(8,128)(2,1)}, bf16[1,8,128,1024]{3,2,0,1:T(8,128)(2,1)S(1)}) fusion(bf16[2,8,128,1024]{3,2,0,1:T(8,128)(2,1)} %bitcast.181), kind=kLoop, calls=%fused_computation.78.clone.1 | loop fusion | bytes 8388608 | tf_op jit(solution)/shard_map/while/body/eval_jaxpr/slice | solution.py:56
  152.5 2.9 copy.46
  155.4 2.8 squeeze.51
  158.2 4.2 %copy.47 = bf16[1,8,128,1024]{2,1,3,0:T(8,128)(2,1)} copy(bf16[1,8,128,1024]{3,2,0,1:T(8,128)(2,1)} %get-tuple-element.435) | data formatting | bytes 4194304 | tf_op jit(solution)/shard_map/while/body/eval_jaxpr/slice | solution.py:56
  162.4 4.2 %squeeze.52 = bf16[1024,16,64]{0,2,1:T(8,128)(2,1)} reshape(bf16[1,8,128,1024]{2,1,3,0:T(8,128)(2,1)} %copy.47) | data formatting | bytes 4194304 | tf_op jit(solution)/shard_map/while/body/eval_jaxpr/reshape;while/body/eval_jaxpr/reshape;while/body/eval_jaxpr/squeeze | solution.py:18
  166.6 2.6 exponential_divide_fusion.2
  169.2 1.7 multiply_convert_fusion.2
  170.8 2.7 fusion.77
  175.9 3.1 copy.48
  178.9 5.4 %copy.49 = f32[8,128,1024]{2,1,0:T(8,128)} copy(f32[8,128,1024]{1,0,2:T(8,128)} %bitcast.183) | data formatting | bytes 8388608 | tf_op jit(solution)/shard_map/while/body/eval_jaxpr/reshape | solution.py:104
  184.4 5.3 %copy.50 = f32[128,8,8,128]{3,2,1,0:T(8,128)} copy(f32[128,8,8,128]{3,1,2,0:T(8,128)} %bitcast.179) | data formatting | bytes 8388608 | tf_op jit(solution)/shard_map/while
  189.6 5.5 %copy.51 = f32[8,128,1024]{2,1,0:T(8,128)} copy(f32[8,128,1024]{1,0,2:T(8,128)} %bitcast.184) | data formatting | bytes 8388608 | tf_op jit(solution)/shard_map/while/body/eval_jaxpr/reshape | solution.py:105
  195.1 9.4 %scatter_fusion = f32[2,10,128,1024]{3,2,1,0:T(8,128)} fusion(f32[2,10,128,1024]{3,2,1,0:T(8,128)} %get-tuple-element.497, s32[8]{0:T(128)S(1)} %select_bitcast_fusion.5, f32[8,128,1024]{2,1,0:T(8,128)} %copy.49), kind=kCustom, calls=%fused_computation.2.clone.clone.1 | custom fusion | flops 1048576 | bytes 12582976 | tf_op jit(solution)/shard_map/while/body/eval_jaxpr/scatter-add | solution.py:104
  204.5 9.5 %scatter_fusion.1 = f32[2,10,128,1024]{3,2,1,0:T(8,128)} fusion(f32[2,10,128,1024]{3,2,1,0:T(8,128)} %scatter_fusion, s32[8]{0:T(128)S(1)} %get-tuple-element.436, f32[8,128,1024]{2,1,0:T(8,128)} %copy.51), kind=kCustom, calls=%fused_computation.3.clone.clone.1 | custom fusion | flops 1048576 | bytes 12582976 | tf_op jit(solution)/shard_map/while/body/eval_jaxpr/scatter-add | solution.py:105
  219.6 5.3 %gather_fusion.1 = bf16[8,2,128,1024]{3,2,1,0:T(8,128)(2,1)} fusion(bf16[2,10,128,1024]{3,2,1,0:T(8,128)(2,1)} %get-tuple-element.520, s32[1024]{0:T(1024)S(1)} %pad_clamp_fusion.5), kind=kCustom, calls=%fused_computation.1.clone.clone.1 | custom fusion | bytes 8388640 | tf_op jit(solution)/shard_map/while/body/eval_jaxpr/gather | solution.py:54
  224.9 4.2 %fusion.76 = (bf16[1,8,128,1024]{3,2,0,1:T(8,128)(2,1)}, bf16[1,8,128,1024]{3,2,0,1:T(8,128)(2,1)S(1)}) fusion(bf16[2,8,128,1024]{3,2,0,1:T(8,128)(2,1)} %bitcast.181), kind=kLoop, calls=%fused_computation.78.clone.1 | loop fusion | bytes 8388608 | tf_op jit(solution)/shard_map/while/body/eval_jaxpr/slice | solution.py:56
  229.1 2.9 copy.46
  232.0 2.8 squeeze.51
  234.9 4.2 %copy.47 = bf16[1,8,128,1024]{2,1,3,0:T(8,128)(2,1)} copy(bf16[1,8,128,1024]{3,2,0,1:T(8,128)(2,1)} %get-tuple-element.435) | data formatting | bytes 4194304 | tf_op jit(solution)/shard_map/while/body/eval_jaxpr/slice | solution.py:56
  239.0 4.2 %squeeze.52 = bf16[1024,16,64]{0,2,1:T(8,128)(2,1)} reshape(bf16[1,8,128,1024]{2,1,3,0:T(8,128)(2,1)} %copy.47) | data formatting | bytes 4194304 | tf_op jit(solution)/shard_map/while/body/eval_jaxpr/reshape;while/body/eval_jaxpr/reshape;while/body/eval_jaxpr/squeeze | solution.py:18
  243.2 2.6 exponential_divide_fusion.2
  245.8 1.7 multiply_convert_fusion.2
  247.5 2.7 fusion.77
  252.5 3.1 copy.48
  255.6 5.4 %copy.49 = f32[8,128,1024]{2,1,0:T(8,128)} copy(f32[8,128,1024]{1,0,2:T(8,128)} %bitcast.183) | data formatting | bytes 8388608 | tf_op jit(solution)/shard_map/while/body/eval_jaxpr/reshape | solution.py:104
  261.0 5.3 %copy.50 = f32[128,8,8,128]{3,2,1,0:T(8,128)} copy(f32[128,8,8,128]{3,1,2,0:T(8,128)} %bitcast.179) | data formatting | bytes 8388608 | tf_op jit(solution)/shard_map/while
  266.3 5.5 %copy.51 = f32[8,128,1024]{2,1,0:T(8,128)} copy(f32[8,128,1024]{1,0,2:T(8,128)} %bitcast.184) | data formatting | bytes 8388608 | tf_op jit(solution)/shard_map/while/body/eval_jaxpr/reshape | solution.py:105
  271.8 9.4 %scatter_fusion = f32[2,10,128,1024]{3,2,1,0:T(8,128)} fusion(f32[2,10,128,1024]{3,2,1,0:T(8,128)} %get-tuple-element.497, s32[8]{0:T(128)S(1)} %select_bitcast_fusion.5, f32[8,128,1024]{2,1,0:T(8,128)} %copy.49), kind=kCustom, calls=%fused_computation.2.clone.clone.1 | custom fusion | flops 1048576 | bytes 12582976 | tf_op jit(solution)/shard_map/while/body/eval_jaxpr/scatter-add | solution.py:104
  281.2 9.5 %scatter_fusion.1 = f32[2,10,128,1024]{3,2,1,0:T(8,128)} fusion(f32[2,10,128,1024]{3,2,1,0:T(8,128)} %scatter_fusion, s32[8]{0:T(128)S(1)} %get-tuple-element.436, f32[8,128,1024]{2,1,0:T(8,128)} %copy.51), kind=kCustom, calls=%fused_computation.3.clone.clone.1 | custom fusion | flops 1048576 | bytes 12582976 | tf_op jit(solution)/shard_map/while/body/eval_jaxpr/scatter-add | solution.py:105
  290.7 4.8 %bitcast_convert_fusion = bf16[2,1280,1024]{2,1,0:T(8,128)(2,1)S(1)} fusion(f32[2,10,128,1024]{3,2,1,0:T(8,128)} %get-tuple-element.130), kind=kLoop, calls=%fused_computation.76 | loop fusion | flops 2621440 | bytes 15728640 | tf_op jit(solution)/shard_map/convert.5
  295.7 2.1 collective-permute-start.4
  297.7 22.3 %collective-permute-done.4 = bf16[2,256,1024]{2,1,0:T(8,128)(2,1)S(1)} collective-permute-done((bf16[2,256,1024]{2,1,0:T(8,128)(2,1)S(1)}, bf16[2,256,1024]{2,1,0:T(8,128)(2,1)S(1)}, u32[]{:S(2)}, u32[]{:S(2)}) %collective-permute-start.4) | collective-permute-done | bytes 1048608 | tf_op jit(solution)/shard_map/ppermute | solution.py:14
  320.1 4.4 %fusion.16 = (bf16[2,256,1024]{2,1,0:T(8,128)(2,1)}, bf16[2,256,1024]{2,1,0:T(8,128)(2,1)}) fusion(f32[2,1280,1024]{2,1,0:T(8,128)} %bitcast.177, bf16[2,256,1024]{2,1,0:T(8,128)(2,1)S(1)} %collective-permute-done.4, bf16[2,256,1024]{2,1,0:T(8,128)(2,1)S(1)} %collective-permute-done.6), kind=kLoop, calls=%fused_computation.51 | loop fusion | flops 3145728 | bytes 8388608 | tf_op jit(solution)/shard_map/convert_element_type | solution.py:127
  324.5 2.5 collective-permute-start.5
  329.0 20.3 %collective-permute-done.5 = bf16[2,256,1024]{2,1,0:T(8,128)(2,1)S(1)} collective-permute-done((bf16[2,256,1024]{2,1,0:T(8,128)(2,1)}, bf16[2,256,1024]{2,1,0:T(8,128)(2,1)S(1)}, u32[]{:S(2)}, u32[]{:S(2)}) %collective-permute-start.5) | collective-permute-done | bytes 1048608 | tf_op jit(solution)/shard_map/ppermute | solution.py:14
  349.3 2.1 fusion.18
  (110 shorter events, 31.7 us)
Async XLA Ops:
  0.6 44.1 %copy-start.11 = (s32[2,8]{1,0:T(2,128)S(1)}, s32[2,8]{1,0:T(2,128)}, u32[]{:S(2)}) copy-start(s32[2,8]{1,0:T(2,128)} %param.14) | copy-start | bytes 196
  0.6 54.5 %copy-start.6 = (bf16[256,1024]{1,0:T(8,128)(2,1)S(1)}, bf16[256,1024]{1,0:T(8,128)(2,1)}, u32[]{:S(2)}) copy-start(bf16[256,1024]{1,0:T(8,128)(2,1)} %param.12) | copy-start | bytes 1572868
  0.7 54.5 %copy-start.7 = (bf16[256,1024]{1,0:T(8,128)(2,1)S(1)}, bf16[256,1024]{1,0:T(8,128)(2,1)}, u32[]{:S(2)}) copy-start(bf16[256,1024]{1,0:T(8,128)(2,1)} %param.11) | copy-start | bytes 1572868
  2.0 25.6 %collective-permute-start = (bf16[2,256,1024]{2,1,0:T(8,128)(2,1)S(1)}, bf16[2,256,1024]{2,1,0:T(8,128)(2,1)}, u32[]{:S(2)}, u32[]{:S(2)}) collective-permute-start(bf16[2,256,1024]{2,1,0:T(8,128)(2,1)S(1)} %pad_maximum_fusion), channel_id=1, source_target_pairs={{0,1},{1,2},{2,3},{3,4},{4,5},{5,6},{6,7},{7,8},{8,9},{9,10},{10,1... | collective-permute-start | bytes 3145736 | tf_op jit(solution)/shard_map/ppermute | solution.py:14
  4.7 36.7 %collective-permute-start.2 = (bf16[2,256,1024]{2,1,0:T(8,128)(2,1)S(1)}, bf16[2,256,1024]{2,1,0:T(8,128)(2,1)S(1)}, u32[]{:S(2)}, u32[]{:S(2)}) collective-permute-start(bf16[2,256,1024]{2,1,0:T(8,128)(2,1)S(1)} %pad_maximum_fusion), channel_id=1, source_target_pairs={{0,15},{1,0},{2,1},{3,2},{4,3},{5,4},{6,5},{7,6},{8,7},{9,8},{10,9... | collective-permute-start | bytes 3145736 | tf_op jit(solution)/shard_map/ppermute | solution.py:14
  27.7 24.8 %collective-permute-start.1 = (bf16[2,256,1024]{2,1,0:T(8,128)(2,1)}, bf16[2,256,1024]{2,1,0:T(8,128)(2,1)}, u32[]{:S(2)}, u32[]{:S(2)}) collective-permute-start(bf16[2,256,1024]{2,1,0:T(8,128)(2,1)} %collective-permute-done), channel_id=1, source_target_pairs={{0,1},{1,2},{2,3},{3,4},{4,5},{5,6},{6,7},{7,8},{8,9},{9,10},{10,1... | collective-permute-start | bytes 3145736 | tf_op jit(solution)/shard_map/ppermute | solution.py:14
  41.4 14.3 %collective-permute-start.3 = (bf16[2,256,1024]{2,1,0:T(8,128)(2,1)S(1)}, bf16[2,256,1024]{2,1,0:T(8,128)(2,1)}, u32[]{:S(2)}, u32[]{:S(2)}) collective-permute-start(bf16[2,256,1024]{2,1,0:T(8,128)(2,1)S(1)} %collective-permute-done.2), channel_id=1, source_target_pairs={{0,15},{1,0},{2,1},{3,2},{4,3},{5,4},{6,5},{7,6},{8,7},{9,8},{10,9... | collective-permute-start | bytes 3145736 | tf_op jit(solution)/shard_map/ppermute | solution.py:14
  53.8 5.6 %copy-start.12 = (s32[2]{0:T(128)S(1)}, s32[2]{0:T(128)}, u32[]{:S(2)}) copy-start(s32[2]{0:T(128)} %param.15) | copy-start | bytes 28
  57.0 2.4 copy-start
  88.5 2.0 copy-start.2
  90.5 2.6 copy-start.3
  93.1 0.8 copy-start.4
  123.0 2.0 copy-start.2
  125.0 2.6 copy-start.3
  127.6 0.8 copy-start.4
  166.6 2.6 copy-start.1
  189.6 5.5 %copy-start.8 = (bf16[2,128,1024]{1,2,0:T(8,128)(2,1)S(1)}, bf16[2,128,1024]{1,2,0:T(8,128)(2,1)}, u32[]{:S(2)}) copy-start(bf16[2,128,1024]{1,2,0:T(8,128)(2,1)} %get-tuple-element.498) | copy-start | bytes 1572868 | tf_op jit(solution)/shard_map/while
  195.1 9.4 %copy-start.9 = (bf16[2,128,1024]{1,2,0:T(8,128)(2,1)}, bf16[2,128,1024]{1,2,0:T(8,128)(2,1)S(1)}, u32[]{:S(2)}) copy-start(bf16[2,128,1024]{1,2,0:T(8,128)(2,1)S(1)} %constant_dynamic-update-slice_fusion.10) | copy-start | bytes 1572868 | tf_op jit(solution)/shard_map/while
  243.2 2.6 copy-start.1
  266.3 5.5 %copy-start.8 = (bf16[2,128,1024]{1,2,0:T(8,128)(2,1)S(1)}, bf16[2,128,1024]{1,2,0:T(8,128)(2,1)}, u32[]{:S(2)}) copy-start(bf16[2,128,1024]{1,2,0:T(8,128)(2,1)} %get-tuple-element.498) | copy-start | bytes 1572868 | tf_op jit(solution)/shard_map/while
  271.8 9.4 %copy-start.9 = (bf16[2,128,1024]{1,2,0:T(8,128)(2,1)}, bf16[2,128,1024]{1,2,0:T(8,128)(2,1)S(1)}, u32[]{:S(2)}) copy-start(bf16[2,128,1024]{1,2,0:T(8,128)(2,1)S(1)} %constant_dynamic-update-slice_fusion.10) | copy-start | bytes 1572868 | tf_op jit(solution)/shard_map/while
  295.7 24.4 %collective-permute-start.4 = (bf16[2,256,1024]{2,1,0:T(8,128)(2,1)S(1)}, bf16[2,256,1024]{2,1,0:T(8,128)(2,1)S(1)}, u32[]{:S(2)}, u32[]{:S(2)}) collective-permute-start(bf16[2,256,1024]{2,1,0:T(8,128)(2,1)S(1)} %get-tuple-element.277), channel_id=1, source_target_pairs={{0,1},{1,2},{2,3},{3,4},{4,5},{5,6},{6,7},{7,8},{8,9},{9,10},{10,1... | collective-permute-start | bytes 3145736 | tf_op jit(solution)/shard_map/ppermute | solution.py:14
  297.7 22.3 %collective-permute-start.6 = (bf16[2,256,1024]{2,1,0:T(8,128)(2,1)S(1)}, bf16[2,256,1024]{2,1,0:T(8,128)(2,1)S(1)}, u32[]{:S(2)}, u32[]{:S(2)}) collective-permute-start(bf16[2,256,1024]{2,1,0:T(8,128)(2,1)S(1)} %get-tuple-element.278), channel_id=1, source_target_pairs={{0,15},{1,0},{2,1},{3,2},{4,3},{5,4},{6,5},{7,6},{8,7},{9,8},{10,9... | collective-permute-start | bytes 3145736 | tf_op jit(solution)/shard_map/ppermute | solution.py:14
  320.1 6.9 %copy-start.5 = (bf16[2,128,1024]{1,2,0:T(8,128)(2,1)S(1)}, bf16[2,128,1024]{1,2,0:T(8,128)(2,1)}, u32[]{:S(2)}) copy-start(bf16[2,128,1024]{1,2,0:T(8,128)(2,1)} %get-tuple-element.126) | copy-start | bytes 1572868
  320.1 7.9 %copy-start.10 = (bf16[2,128,1024]{1,2,0:T(8,128)(2,1)S(1)}, bf16[2,128,1024]{1,2,0:T(8,128)(2,1)}, u32[]{:S(2)}) copy-start(bf16[2,128,1024]{1,2,0:T(8,128)(2,1)} %get-tuple-element.129) | copy-start | bytes 1572868
  324.5 24.8 %collective-permute-start.5 = (bf16[2,256,1024]{2,1,0:T(8,128)(2,1)}, bf16[2,256,1024]{2,1,0:T(8,128)(2,1)S(1)}, u32[]{:S(2)}, u32[]{:S(2)}) collective-permute-start(bf16[2,256,1024]{2,1,0:T(8,128)(2,1)} %get-tuple-element.275), channel_id=1, source_target_pairs={{0,1},{1,2},{2,3},{3,4},{4,5},{5,6},{6,7},{7,8},{8,9},{9,10},{10,1... | collective-permute-start | bytes 3145736 | tf_op jit(solution)/shard_map/ppermute | solution.py:14
  327.0 22.3 %collective-permute-start.7 = (bf16[2,256,1024]{2,1,0:T(8,128)(2,1)}, bf16[2,256,1024]{2,1,0:T(8,128)(2,1)S(1)}, u32[]{:S(2)}, u32[]{:S(2)}) collective-permute-start(bf16[2,256,1024]{2,1,0:T(8,128)(2,1)} %get-tuple-element.276), channel_id=1, source_target_pairs={{0,15},{1,0},{2,1},{3,2},{4,3},{5,4},{6,5},{7,6},{8,7},{9,8},{10,9... | collective-permute-start | bytes 3145736 | tf_op jit(solution)/shard_map/ppermute | solution.py:14
where the time goes:
time: 354 us; the launch traced here: 352 us
  local copies, waits for them, and re-layouts  161 us (45%)
  waiting for transfers between devices  85 us (24%)
  other arithmetic  58.6 us (17%)
  matrix products  26.4 us (7%)
  loops' own time  11.1 us (3%)
  starting transfers between devices  9.82 us (3%)
    ppermute x8, waiting for transfers between devices, shifted(): lax.ppermute(x, axis, [(i, (i + by) % length) for i in range(length)])  85 us
    squeeze x8, local copies, waits for them, and re-layouts, split_heads(): return matrix.reshape(matrix.shape[0], HEADS, matrix.shape[1] // HEADS)  24.3 us
    slice x6, local copies, waits for them, and re-layouts, block_inputs(): k_all = split_heads(picked[0].reshape(list_width * blk_len, model_width))  23.7 us
    slice x6, local copies, waits for them, and re-layouts, block_inputs(): v_all = split_heads(picked[1].reshape(list_width * blk_len, model_width))  23.6 us
    gather x4, local copies, waits for them, and re-layouts, block_inputs(): picked = window_tiles[:, slots]  21 us
    scatter-add x2, other arithmetic, outer_step(): grad_win.at[1, slots].add(dv_all.reshape(list_width, blk_len, model_width))  19 us
    scatter-add x2, other arithmetic, outer_step(): grad_win.at[0, slots].add(dk_all.reshape(list_width, blk_len, model_width))  18.8 us
    while x28, local copies, waits for them, and re-layouts  18.3 us
  transfers between devices with their start and end apart: 8, of which 6 were waited for; matrix products, arithmetic and copies ran while one was open for 2% of the time, Pallas kernels for 0%

commit v1 on v0

v1 whole, which is shorter than its diff:
```python
import functools
import math

import jax
import jax.numpy as jnp
from jax import lax
from jax.experimental import pallas as pl
from jax.experimental.pallas import tpu as pltpu
from jax.sharding import PartitionSpec as P

HEADS = 16
LANES = 128
F32 = jnp.float32
BF16 = jnp.bfloat16
VMEM = pl.BlockSpec(memory_space=pltpu.VMEM)
SMEM = pl.BlockSpec(memory_space=pltpu.SMEM)


def permuted(x, target):
    length = lax.axis_size("blk")
    return lax.ppermute(x, "blk", [(i, target(i) % length) for i in range(length)])


def core_swap(x):
    return permuted(x, lambda i: i ^ 1)


def pair_swap(x):
    return permuted(x, lambda i: i ^ 2)


def relay(x, sign):
    return permuted(x, lambda i: i + sign * 4 if (i & 2) == 0 else i - sign * 4)


def dot(a, b):
    return jnp.dot(a, b, preferred_element_type=F32)


def pack_body(core_ref, a_ref, b_ref, keep_ref, send_ref):
    core = core_ref[0]
    chunks, _, rows, lanes = keep_ref.shape
    half = chunks * lanes
    for index, ref in enumerate((a_ref, b_ref)):
        for chunk in range(chunks):
            mine = pl.multiple_of(core * half + chunk * lanes, lanes)
            other = pl.multiple_of((1 - core) * half + chunk * lanes, lanes)
            keep_ref[chunk, index] = ref[:, pl.ds(mine, lanes)]
            send_ref[chunk, index] = ref[:, pl.ds(other, lanes)]


def pack(core, a, b):
    rows, width = a.shape
    chunks = width // 2 // LANES
    shape = jax.ShapeDtypeStruct((chunks, 2, rows, LANES), a.dtype)
    return pl.pallas_call(
        pack_body,
        out_shape=(shape, shape),
        in_specs=[SMEM, VMEM, VMEM],
        out_specs=(VMEM, VMEM),
        name="pack",
    )(core, a, b)


def zip_body(keep_ref, recv_ref, *out_refs):
    for chunk, out_ref in enumerate(out_refs):
        out_ref[0] = keep_ref[chunk]
        out_ref[1] = recv_ref[chunk]


def zip_chunks(keep, recv):
    shape = jax.ShapeDtypeStruct((2,) + keep.shape[1:], keep.dtype)
    return pl.pallas_call(
        zip_body,
        out_shape=(shape,) * keep.shape[0],
        in_specs=[VMEM, VMEM],
        out_specs=(VMEM,) * keep.shape[0],
        name="zip",
    )(keep, recv)


def unpack_body(core_ref, *refs):
    core = core_ref[0]
    a_ref, b_ref = refs[-2:]
    chunks = (len(refs) - 2) // 2
    lanes = refs[0].shape[2]
    half = chunks * lanes
    for index, ref in enumerate((a_ref, b_ref)):
        for chunk in range(chunks):
            mine = pl.multiple_of(core * half + chunk * lanes, lanes)
            other = pl.multiple_of((1 - core) * half + chunk * lanes, lanes)
            ref[:, pl.ds(mine, lanes)] = refs[chunk][index]
            ref[:, pl.ds(other, lanes)] = refs[chunks + chunk][index]


def unpack(core, keep, recv):
    chunks = len(keep)
    _, rows, lanes = keep[0].shape
    shape = jax.ShapeDtypeStruct((rows, 2 * chunks * lanes), keep[0].dtype)
    return pl.pallas_call(
        unpack_body,
        out_shape=(shape, shape),
        in_specs=[SMEM] + [VMEM] * (2 * chunks),
        out_specs=(VMEM, VMEM),
        name="unpack",
    )(core, *keep, *recv)


def attend_body(
    slots,
    counts,
    qg_keep,
    qg_recv,
    kv_own,
    kv_pair,
    kv_far,
    od_keep,
    od_send,
    g_own,
    g_pair,
    g_far,
    kw,
    vw,
    kt,
    vt,
    dk,
    dv,
    scores,
    expd,
    mt,
    lt,
    ot,
    dqt,
):
    blk = kw.shape[1]
    own_blocks = kv_own.shape[2] // blk
    chip_blocks = 2 * own_blocks
    list_width = slots.shape[0] // chip_blocks
    head_dim = LANES // 2
    factor = 1.0 / math.sqrt(head_dim)
    for buf, ref in enumerate((kv_own, kv_pair, kv_far)):
        for src in range(2):
            for b in range(own_blocks):
                index = buf * chip_blocks + src * own_blocks + b
                k_tile = ref[src, 0, b * blk : (b + 1) * blk, :]
                v_tile = ref[src, 1, b * blk : (b + 1) * blk, :]
                kw[index] = k_tile
                vw[index] = v_tile
                kt[index] = k_tile.T
                vt[index] = v_tile.T
    dk[...] = jnp.zeros_like(dk)
    dv[...] = jnp.zeros_like(dv)
    row_ids = lax.broadcasted_iota(jnp.int32, (LANES, blk), 0)
    first_rows = row_ids < head_dim

    def lanes_first():
        return lax.broadcasted_iota(jnp.int32, (blk, LANES), 1) < head_dim

    def diagonal_t(tile_t):
        zero = jnp.zeros_like(tile_t)
        return jnp.concatenate(
            [jnp.where(first_rows, tile_t, zero), jnp.where(first_rows, zero, tile_t)], axis=1
        )

    def diagonal(tile):
        zero = jnp.zeros_like(tile)
        first = lanes_first()
        return jnp.concatenate([jnp.where(first, tile, zero), jnp.where(first, zero, tile)], axis=0)

    def collapse(wide):
        return jnp.where(first_rows, wide[:, :blk], wide[:, blk:])

    for row_block in range(chip_blocks):
        src, b = divmod(row_block, own_blocks)
        source = (qg_keep, qg_recv)[src]
        rows = slice(b * blk, (b + 1) * blk)
        q_tile = source[0, 0, rows, :].astype(F32) * factor
        g_tile = source[0, 1, rows, :].astype(F32)
        q_diag_t = diagonal_t(q_tile.T).astype(BF16)
        q_diag = diagonal(q_tile).astype(BF16)
        g_diag_t = diagonal_t(g_tile.T)
        count = counts[row_block]
        names = [slots[row_block * list_width + s] for s in range(list_width)]

        def gated(j, body):
            if j == 0:
                body()
            else:
                pl.when(2 * j < count)(body)

        def score_step(j):
            def body():
                s0, s1 = names[2 * j], names[2 * j + 1]
                top = dot(kw[s0], q_diag_t)
                low = dot(kw[s1], q_diag_t)
                low = jnp.where(2 * j + 1 < count, low, -jnp.inf)
                scores[j, :blk] = top
                scores[j, blk:] = low
                both = jnp.maximum(top, low).reshape(blk // 8, 8, 2 * blk)
                best = jnp.max(both, axis=0)
                mt[...] = best if j == 0 else jnp.maximum(mt[...], best)

            return body

        for j in range(list_width // 2):
            gated(j, score_step(j))
        row_max = jnp.max(mt[...], axis=0, keepdims=True)

        def value_step(j):
            def body():
                s0, s1 = names[2 * j], names[2 * j + 1]
                e = jnp.exp(scores[j] - row_max)
                part = jnp.sum(e.reshape(2 * blk // 8, 8, 2 * blk), axis=0)
                lt[...] = part if j == 0 else lt[...] + part
                e_bf = e.astype(BF16)
                expd[j] = e_bf
                v_t = jnp.concatenate([vt[s0], vt[s1]], axis=1)
                mixed = dot(v_t, e_bf)
                ot[...] = mixed if j == 0 else ot[...] + mixed

            return body

        for j in range(list_width // 2):
            gated(j, value_step(j))
        inverse = 1.0 / jnp.sum(lt[...], axis=0, keepdims=True)
        out_t = ot[...] * inverse
        out_rounded = out_t.astype(BF16).astype(F32)
        g_scaled_t = g_diag_t * inverse
        delta = jnp.sum(g_scaled_t * out_rounded, axis=0, keepdims=True)
        g_t_bf = g_scaled_t.astype(BF16)
        g_bf = g_scaled_t.T.astype(BF16)
        out_ref = (od_keep, od_send)[src]
        out_ref[0, rows, :] = collapse(out_t).T.astype(BF16)

        def grad_step(j):
            def body():
                s0, s1 = names[2 * j], names[2 * j + 1]
                e_bf = expd[j]
                v_both = jnp.concatenate([vw[s0], vw[s1]], axis=0)
                dp = dot(v_both, g_t_bf)
                ds = (e_bf.astype(F32) * (dp - delta)).astype(BF16)
                k_t = jnp.concatenate([kt[s0], kt[s1]], axis=1)
                moved = dot(k_t, ds)
                dqt[...] = moved if j == 0 else dqt[...] + moved
                dv_both = dot(e_bf, g_bf)
                dk_both = dot(ds, q_diag)
                dv[s0] += dv_both[:blk]
                dv[s1] += dv_both[blk:]
                dk[s0] += dk_both[:blk]
                dk[s1] += dk_both[blk:]

            return body

        for j in range(list_width // 2):
            gated(j, grad_step(j))
        out_ref[1, rows, :] = (collapse(dqt[...]) * factor).T.astype(BF16)

    for buf, ref in enumerate((g_own, g_pair, g_far)):
        for src in range(2):
            for b in range(own_blocks):
                index = buf * chip_blocks + src * own_blocks + b
                ref[src, 0, b * blk : (b + 1) * blk, :] = dk[index].astype(ref.dtype)
                ref[src, 1, b * blk : (b + 1) * blk, :] = dv[index].astype(ref.dtype)


def attend(chunk, slots, counts, qg_keep, qg_recv, kv_own, kv_pair, kv_far, blk):
    rows = kv_own.shape[2]
    chip_blocks = 2 * rows // blk
    window = 3 * chip_blocks
    list_width = slots.shape[0] // chip_blocks
    pairs = list_width // 2
    column = pl.BlockSpec((1, 2, rows, LANES), lambda i: (chunk, 0, 0, 0))
    whole = pl.BlockSpec((2, 2, rows, LANES), lambda i: (0, 0, 0, 0))
    flat = pl.BlockSpec((2, rows, LANES), lambda i: (0, 0, 0))
    units = chip_blocks * list_width
    return pl.pallas_call(
        attend_body,
        grid=(1,),
        out_shape=(
            jax.ShapeDtypeStruct((2, rows, LANES), BF16),
            jax.ShapeDtypeStruct((2, rows, LANES), BF16),
            jax.ShapeDtypeStruct((2, 2, rows, LANES), F32),
            jax.ShapeDtypeStruct((2, 2, rows, LANES), F32),
            jax.ShapeDtypeStruct((2, 2, rows, LANES), BF16),
        ),
        in_specs=[SMEM, SMEM, column, column, whole, whole, whole],
        out_specs=(flat, flat, whole, whole, whole),
        scratch_shapes=[
            pltpu.VMEM((window, blk, LANES), BF16),
            pltpu.VMEM((window, blk, LANES), BF16),
            pltpu.VMEM((window, LANES, blk), BF16),
            pltpu.VMEM((window, LANES, blk), BF16),
            pltpu.VMEM((window, blk, LANES), F32),
            pltpu.VMEM((window, blk, LANES), F32),
            pltpu.VMEM((pairs, 2 * blk, 2 * blk), F32),
            pltpu.VMEM((pairs, 2 * blk, 2 * blk), BF16),
            pltpu.VMEM((8, 2 * blk), F32),
            pltpu.VMEM((8, 2 * blk), F32),
            pltpu.VMEM((LANES, 2 * blk), F32),
            pltpu.VMEM((LANES, 2 * blk), F32),
        ],
        cost_estimate=pl.CostEstimate(
            flops=units * 24 * blk * blk * LANES,
            transcendentals=units * 2 * blk * blk,
            bytes_accessed=16 * rows * LANES * 4,
        ),
        name="attend",
    )(slots, counts, qg_keep, qg_recv, kv_own, kv_pair, kv_far)


def local(query, key_in, value, grad_out, neighbors, counts):
    rows, width = query.shape
    own_blocks, list_width = neighbors.shape
    blk = rows // own_blocks
    chunks = width // 2 // LANES
    shard_count = lax.axis_size("blk")
    shard_index = lax.axis_index("blk")
    core = shard_index % 2
    core_arr = core.astype(jnp.int32).reshape(1)

    kv_keep, kv_send = pack(core_arr, key_in, value)
    kv_recv = core_swap(kv_send)
    lists = jnp.concatenate([neighbors, counts[:, None]], axis=1)
    lists = jnp.concatenate([lists, core_swap(lists)], axis=0)
    qg_keep, qg_send = pack(core_arr, query, grad_out)
    qg_recv = core_swap(qg_send)

    home = lists[:, :list_width] // own_blocks
    step = jnp.mod(home // 2 - shard_index // 2 + 1, shard_count // 2)
    pair_step = jnp.where((shard_index // 2) % 2 == 0, 2, 0)
    buf = jnp.where(step == 1, 0, jnp.where(step == pair_step, 1, 2))
    place = (home % 2) ^ core
    slots = (buf * 2 + place) * own_blocks + lists[:, :list_width] % own_blocks
    slots = slots.astype(jnp.int32).reshape(-1)
    used = lists[:, list_width]

    kv_own = zip_chunks(kv_keep, kv_recv)
    kv_pair = [pair_swap(kv_own[c]) for c in range(chunks)]
    kv_far = [relay(kv_pair[c], 1) for c in range(chunks)]
    mine, theirs, grad_mine, grad_theirs = [], [], [], []
    for c in range(chunks):
        od_keep, od_send, g_own, g_pair, g_far = attend(
            c, slots, used, qg_keep, qg_recv, kv_own[c], kv_pair[c], kv_far[c], blk
        )
        mine.append(od_keep)
        theirs.append(od_send)
        back = relay(g_far, -1)
        total = (g_pair + back.astype(F32)).astype(BF16)
        back = pair_swap(total)
        total = (g_own + back.astype(F32)).astype(BF16)
        grad_mine.append(total[0])
        grad_theirs.append(total[1])
    got = core_swap(jnp.stack(theirs))
    attn_out, grad_query = unpack(core_arr, mine, [got[c] for c in range(chunks)])
    got = core_swap(jnp.stack(grad_theirs))
    grad_key, grad_value = unpack(core_arr, grad_mine, [got[c] for c in range(chunks)])
    return (attn_out, grad_query, grad_key, grad_value)


def solution(mesh):
    spec = P(("groups", "blk"), None)
    flat = P(("groups", "blk"))
    return jax.shard_map(
        local,
        mesh=mesh,
        in_specs=(spec, spec, spec, spec, spec, flat),
        out_specs=(spec, spec, spec, spec),
        check_vma=False,
    )
```

time: 354 us -> 140 us (0.40)
  local copies, waits for them, and re-layouts: 161 us -> 11.7 us
  Pallas kernels: 0 us -> 65.9 us
  other arithmetic: 58.6 us -> 1.77 us
  waiting for transfers between devices: 85 us -> 32.8 us
  matrix products: 26.4 us -> 0 us
  starting transfers between devices: 9.82 us -> 26.8 us
  loops' own time: 11.1 us -> 0 us
    pallas_call x0 -> x9, Pallas kernels: none -> 65.9 us  [the longest x4 53.8 us: attend(): pl.pallas_call(attend_body, grid=(1,), out_shape=(jax.ShapeDtypeStruct((2...]
    ppermute x8 -> x21, waiting for transfers between devices: 85 us -> 32.8 us  [permuted(): lax.ppermute(x, 'blk', [(i, target(i) % length) for i in range(length)])]
    slice x13 -> x5, local copies, waits for them, and re-layouts: 47.5 us -> 3.41 us  [the longest x4 2.66 us: local(): grad_theirs.append(total[1])]
    scatter-add x4 -> x0, other arithmetic: 37.8 us -> none  [the longest x2 19 us: outer_step(): grad_win.at[1, slots].add(dv_all.reshape(list_width, blk_len, model_width))]
    dot_general x14 -> x0, matrix products: 26.4 us -> none  [the longest x4 7.93 us: block_inputs(): jnp.einsum('qhd,khd->hqk', q_tile, k_all, preferred_element_type=jnp.floa...]
    squeeze x8 -> x2, local copies, waits for them, and re-layouts: 24.3 us -> 1.61 us  [local(): got[c]]
    reshape x4 -> x1, local copies, waits for them, and re-layouts: 21.8 us -> 0.62 us  [local(): slots = slots.astype(jnp.int32).reshape(-1)]
    gather x4 -> x0, local copies, waits for them, and re-layouts: 21 us -> none  [block_inputs(): picked = window_tiles[:, slots]]
  transfers between devices with their start and end apart: 8 -> 21, of which waited for: 6 -> 9; matrix products, arithmetic and copies ran while one was open for 2% -> 5% of each run, Pallas kernels for 0% -> 42%
where the time goes in v1:
time: 140 us
  Pallas kernels  65.9 us (47%)
  waiting for transfers between devices  32.8 us (23%)
  starting transfers between devices  26.8 us (19%)
  local copies, waits for them, and re-layouts  11.7 us (8%)
  other arithmetic  1.77 us (1%)
    pallas_call x4, Pallas kernels, attend(): pl.pallas_call(attend_body, grid=(1,), out_shape=(jax.ShapeDtypeStruct((2...  53.8 us
    ppermute x21, waiting for transfers between devices, permuted(): lax.ppermute(x, 'blk', [(i, target(i) % length) for i in range(length)])  32.8 us
    ppermute x21, starting transfers between devices, permuted(): lax.ppermute(x, 'blk', [(i, target(i) % length) for i in range(length)])  26.8 us
    unnamed x52, local copies, waits for them, and re-layouts  5.97 us
    pallas_call x2, Pallas kernels, unpack(): pl.pallas_call(unpack_body, out_shape=(shape, shape), in_specs=[SMEM] + [...  5.1 us
    pallas_call x2, Pallas kernels, pack(): pl.pallas_call(pack_body, out_shape=(shape, shape), in_specs=[SMEM, VMEM,...  4.87 us
  transfers between devices with their start and end apart: 21, of which 9 were waited for; matrix products, arithmetic and copies ran while one was open for 5% of the time, Pallas kernels for 42%

profile of v1, /device:TPU:1, one launch (start us, length us, event | category | flops | bytes accessed | tf_op | source)
XLA Modules:
  0.0 139.8 jit_solution(9342732156293207998)
XLA Ops:
  0.6 2.4 %pack.3 = (bf16[4,2,256,128]{3,2,1,0:T(8,128)(2,1)}, bf16[4,2,256,128]{3,2,1,0:T(8,128)(2,1)}) custom-call(s32[1]{0:T(128)} %bitcast.core_ref, bf16[256,1024]{1,0:T(8,128)(2,1)} %a_ref.3, bf16[256,1024]{1,0:T(8,128)(2,1)} %b_ref.3), custom_call_target="tpu_custom_call" | custom-call | tf_op jit(solution)/shard_map/pack/pallas_call | solution.py:56
  3.1 2.1 %collective-permute-done.2.recv_ref = bf16[4,2,256,128]{3,2,1,0:T(8,128)(2,1)S(1)} collective-permute-done((bf16[4,2,256,128]{3,2,1,0:T(8,128)(2,1)}, bf16[4,2,256,128]{3,2,1,0:T(8,128)(2,1)S(1)}, u32[]{:S(2)}, u32[]{:S(2)}) %collective-permute-start.2) | collective-permute-done | bytes 524320 | tf_op jit(solution)/shard_map/ppermute | solution.py:21
  5.2 0.8 copy-done.8
  6.0 2.2 %zip.1 = (bf16[2,2,256,128]{3,2,1,0:T(8,128)(2,1)}, bf16[2,2,256,128]{3,2,1,0:T(8,128)(2,1)}, bf16[2,2,256,128]{3,2,1,0:T(8,128)(2,1)}, bf16[2,2,256,128]{3,2,1,0:T(8,128)(2,1)}) custom-call(bf16[4,2,256,128]{3,2,1,0:T(8,128)(2,1)} %get-tuple-element.38.keep_ref, bf16[4,2,256,128]{3,2,1,0:T(8,128)(2,1)} %copy-done.8), custom_call_target="tpu_custom_call" | custom-call | tf_op jit(solution)/shard_map/zip/pallas_call | solution.py:73
  8.2 2.4 %collective-permute-start.9 = (bf16[2,2,256,128]{3,2,1,0:T(8,128)(2,1)}, bf16[2,2,256,128]{3,2,1,0:T(8,128)(2,1)S(1)}, u32[]{:S(2)}, u32[]{:S(2)}) collective-permute-start(bf16[2,2,256,128]{3,2,1,0:T(8,128)(2,1)} %get-tuple-element.46.kv_own), channel_id=1, source_target_pairs={{0,2},{1,3},{2,0},{3,1},{4,6},{5,7},{6,4},{7,5},{8,10},{9,11},{10,... | collective-permute-start | bytes 786440 | tf_op jit(solution)/shard_map/ppermute | solution.py:21
  10.6 2.4 %pack.2 = (bf16[4,2,256,128]{3,2,1,0:T(8,128)(2,1)}, bf16[4,2,256,128]{3,2,1,0:T(8,128)(2,1)}) custom-call(s32[1]{0:T(128)} %bitcast.core_ref, bf16[256,1024]{1,0:T(8,128)(2,1)} %a_ref.2, bf16[256,1024]{1,0:T(8,128)(2,1)} %b_ref.2), custom_call_target="tpu_custom_call" | custom-call | tf_op jit(solution)/shard_map/pack/pallas_call | solution.py:56
  13.0 0.7 collective-permute-start.1
  13.7 0.1 copy.11
  13.8 0.6 copy-done.12
  14.4 0.1 pad_add_fusion.1
  14.5 0.7 collective-permute-start
  15.1 0.8 collective-permute-done
  15.9 0.1 pad_add_fusion
  16.0 0.7 collective-permute-start.5
  16.7 0.8 collective-permute-start.3
  17.5 1.3 collective-permute-start.10
  18.8 0.6 reshape.15.slots
  19.4 3.5 %collective-permute-done.7.kv_pair = bf16[2,2,256,128]{3,2,1,0:T(8,128)(2,1)S(1)} collective-permute-done((bf16[2,2,256,128]{3,2,1,0:T(8,128)(2,1)S(1)}, bf16[2,2,256,128]{3,2,1,0:T(8,128)(2,1)S(1)}, u32[]{:S(2)}, u32[]{:S(2)}) %collective-permute-start.7) | collective-permute-done | bytes 262176 | tf_op jit(solution)/shard_map/ppermute | solution.py:21
  22.9 1.5 %collective-permute-start.8 = (bf16[2,2,256,128]{3,2,1,0:T(8,128)(2,1)S(1)}, bf16[2,2,256,128]{3,2,1,0:T(8,128)(2,1)S(1)}, u32[]{:S(2)}, u32[]{:S(2)}) collective-permute-start(bf16[2,2,256,128]{3,2,1,0:T(8,128)(2,1)S(1)} %collective-permute-done.7.kv_pair), channel_id=1, source_target_pairs={{0,4},{1,5},{2,14},{3,15},{4,8},{5,9},{6,2},{7,3},{8,12},{9,13},{1... | collective-permute-start | bytes 786440 | tf_op jit(solution)/shard_map/ppermute | solution.py:21
  24.4 0.7 slice_reduce_fusion.counts
  25.2 3.4 %collective-permute-done.5.kv_pair = bf16[2,2,256,128]{3,2,1,0:T(8,128)(2,1)S(1)} collective-permute-done((bf16[2,2,256,128]{3,2,1,0:T(8,128)(2,1)S(1)}, bf16[2,2,256,128]{3,2,1,0:T(8,128)(2,1)S(1)}, u32[]{:S(2)}, u32[]{:S(2)}) %collective-permute-start.5) | collective-permute-done | bytes 262176 | tf_op jit(solution)/shard_map/ppermute | solution.py:21
  28.6 1.5 %collective-permute-start.6 = (bf16[2,2,256,128]{3,2,1,0:T(8,128)(2,1)S(1)}, bf16[2,2,256,128]{3,2,1,0:T(8,128)(2,1)S(1)}, u32[]{:S(2)}, u32[]{:S(2)}) collective-permute-start(bf16[2,2,256,128]{3,2,1,0:T(8,128)(2,1)S(1)} %collective-permute-done.5.kv_pair), channel_id=1, source_target_pairs={{0,4},{1,5},{2,14},{3,15},{4,8},{5,9},{6,2},{7,3},{8,12},{9,13},{1... | collective-permute-start | bytes 786440 | tf_op jit(solution)/shard_map/ppermute | solution.py:21
  30.0 4.1 %collective-permute-done.3.kv_pair = bf16[2,2,256,128]{3,2,1,0:T(8,128)(2,1)S(1)} collective-permute-done((bf16[2,2,256,128]{3,2,1,0:T(8,128)(2,1)S(1)}, bf16[2,2,256,128]{3,2,1,0:T(8,128)(2,1)S(1)}, u32[]{:S(2)}, u32[]{:S(2)}) %collective-permute-start.3) | collective-permute-done | bytes 262176 | tf_op jit(solution)/shard_map/ppermute | solution.py:21
  34.2 1.5 %collective-permute-start.4 = (bf16[2,2,256,128]{3,2,1,0:T(8,128)(2,1)S(1)}, bf16[2,2,256,128]{3,2,1,0:T(8,128)(2,1)S(1)}, u32[]{:S(2)}, u32[]{:S(2)}) collective-permute-start(bf16[2,2,256,128]{3,2,1,0:T(8,128)(2,1)S(1)} %collective-permute-done.3.kv_pair), channel_id=1, source_target_pairs={{0,4},{1,5},{2,14},{3,15},{4,8},{5,9},{6,2},{7,3},{8,12},{9,13},{1... | collective-permute-start | bytes 786440 | tf_op jit(solution)/shard_map/ppermute | solution.py:21
  35.7 0.8 copy-done.13
  36.4 0.1 copy-done.24
  36.5 13.4 %attend.7 = (bf16[2,256,128]{2,1,0:T(8,128)(2,1)}, bf16[2,256,128]{2,1,0:T(8,128)(2,1)}, f32[2,2,256,128]{3,2,1,0:T(8,128)}, f32[2,2,256,128]{3,2,1,0:T(8,128)}, bf16[2,2,256,128]{3,2,1,0:T(8,128)(2,1)}) custom-call(s32[32]{0:T(128)} %reshape.15.slots, s32[4]{0:T(128)} %slice_reduce_fusion.counts, bf16[4,2,256,128]{3,2,1,0:T(8,128)(2,1)} %get-tuple-element.36.qg_keep, ...), custom_call_target="tpu_custom_call" | custom-call | flops 1610612736 | bytes 2097152 | tf_op jit(solution)/shard_map/attend/pallas_call | solution.py:276
  49.9 4.4 %collective-permute-start.18 = (bf16[2,2,256,128]{3,2,1,0:T(8,128)(2,1)}, bf16[2,2,256,128]{3,2,1,0:T(8,128)(2,1)S(1)}, u32[]{:S(2)}, u32[]{:S(2)}) collective-permute-start(bf16[2,2,256,128]{3,2,1,0:T(8,128)(2,1)} %get-tuple-element.65), channel_id=1, source_target_pairs={{0,12},{1,13},{2,6},{3,7},{4,0},{5,1},{6,10},{7,11},{8,4},{9,5},{1... | collective-permute-start | bytes 786440 | tf_op jit(solution)/shard_map/ppermute | solution.py:21
  54.3 0.7 copy-done.23
  55.0 13.5 %attend.6 = (bf16[2,256,128]{2,1,0:T(8,128)(2,1)}, bf16[2,256,128]{2,1,0:T(8,128)(2,1)}, f32[2,2,256,128]{3,2,1,0:T(8,128)}, f32[2,2,256,128]{3,2,1,0:T(8,128)}, bf16[2,2,256,128]{3,2,1,0:T(8,128)(2,1)}) custom-call(s32[32]{0:T(128)} %reshape.15.slots, s32[4]{0:T(128)} %slice_reduce_fusion.counts, bf16[4,2,256,128]{3,2,1,0:T(8,128)(2,1)} %get-tuple-element.36.qg_keep, ...), custom_call_target="tpu_custom_call" | custom-call | flops 1610612736 | bytes 2097152 | tf_op jit(solution)/shard_map/attend/pallas_call | solution.py:276
  68.6 2.3 %collective-permute-start.16 = (bf16[2,2,256,128]{3,2,1,0:T(8,128)(2,1)}, bf16[2,2,256,128]{3,2,1,0:T(8,128)(2,1)S(1)}, u32[]{:S(2)}, u32[]{:S(2)}) collective-permute-start(bf16[2,2,256,128]{3,2,1,0:T(8,128)(2,1)} %get-tuple-element.62), channel_id=1, source_target_pairs={{0,12},{1,13},{2,6},{3,7},{4,0},{5,1},{6,10},{7,11},{8,4},{9,5},{1... | collective-permute-start | bytes 786440 | tf_op jit(solution)/shard_map/ppermute | solution.py:21
  70.9 0.7 copy-done.22
  71.6 13.6 %attend.5 = (bf16[2,256,128]{2,1,0:T(8,128)(2,1)}, bf16[2,256,128]{2,1,0:T(8,128)(2,1)}, f32[2,2,256,128]{3,2,1,0:T(8,128)}, f32[2,2,256,128]{3,2,1,0:T(8,128)}, bf16[2,2,256,128]{3,2,1,0:T(8,128)(2,1)}) custom-call(s32[32]{0:T(128)} %reshape.15.slots, s32[4]{0:T(128)} %slice_reduce_fusion.counts, bf16[4,2,256,128]{3,2,1,0:T(8,128)(2,1)} %get-tuple-element.36.qg_keep, ...), custom_call_target="tpu_custom_call" | custom-call | flops 1610612736 | bytes 2097152 | tf_op jit(solution)/shard_map/attend/pallas_call | solution.py:276
  85.2 2.4 %collective-permute-start.14 = (bf16[2,2,256,128]{3,2,1,0:T(8,128)(2,1)}, bf16[2,2,256,128]{3,2,1,0:T(8,128)(2,1)S(1)}, u32[]{:S(2)}, u32[]{:S(2)}) collective-permute-start(bf16[2,2,256,128]{3,2,1,0:T(8,128)(2,1)} %get-tuple-element.59), channel_id=1, source_target_pairs={{0,12},{1,13},{2,6},{3,7},{4,0},{5,1},{6,10},{7,11},{8,4},{9,5},{1... | collective-permute-start | bytes 786440 | tf_op jit(solution)/shard_map/ppermute | solution.py:21
  87.5 0.7 copy-done.21
  88.3 13.3 %attend.4 = (bf16[2,256,128]{2,1,0:T(8,128)(2,1)}, bf16[2,256,128]{2,1,0:T(8,128)(2,1)}, f32[2,2,256,128]{3,2,1,0:T(8,128)}, f32[2,2,256,128]{3,2,1,0:T(8,128)}, bf16[2,2,256,128]{3,2,1,0:T(8,128)(2,1)}) custom-call(s32[32]{0:T(128)} %reshape.15.slots, s32[4]{0:T(128)} %slice_reduce_fusion.counts, bf16[4,2,256,128]{3,2,1,0:T(8,128)(2,1)} %get-tuple-element.36.qg_keep, ...), custom_call_target="tpu_custom_call" | custom-call | flops 1610612736 | bytes 2097152 | tf_op jit(solution)/shard_map/attend/pallas_call | solution.py:276
  101.6 2.3 %collective-permute-start.12 = (bf16[2,2,256,128]{3,2,1,0:T(8,128)(2,1)}, bf16[2,2,256,128]{3,2,1,0:T(8,128)(2,1)S(1)}, u32[]{:S(2)}, u32[]{:S(2)}) collective-permute-start(bf16[2,2,256,128]{3,2,1,0:T(8,128)(2,1)} %get-tuple-element.56), channel_id=1, source_target_pairs={{0,12},{1,13},{2,6},{3,7},{4,0},{5,1},{6,10},{7,11},{8,4},{9,5},{1... | collective-permute-start | bytes 786440 | tf_op jit(solution)/shard_map/ppermute | solution.py:21
  103.9 1.0 pad_maximum_fusion
  104.9 1.6 %collective-permute-start.11 = (bf16[4,2,256,128]{3,2,1,0:T(8,128)(2,1)S(1)}, bf16[4,2,256,128]{3,2,1,0:T(8,128)(2,1)S(1)}, u32[]{:S(2)}, u32[]{:S(2)}) collective-permute-start(bf16[4,2,256,128]{3,2,1,0:T(8,128)(2,1)S(1)} %pad_maximum_fusion), channel_id=1, source_target_pairs={{0,1},{1,0},{2,3},{3,2},{4,5},{5,4},{6,7},{7,6},{8,9},{9,8},{10,11... | collective-permute-start | bytes 1572872 | tf_op jit(solution)/shard_map/ppermute | solution.py:21
  106.5 0.1 add_convert_fusion.1
  106.6 0.1 collective-permute-start.19
  106.7 0.9 copy-done.5
  107.6 0.1 add_convert_fusion.3
  107.6 0.6 collective-permute-start.17
  108.3 0.3 copy-done.6
  108.6 0.1 add_convert_fusion.5
  108.7 0.6 collective-permute-start.15
  109.3 0.3 copy-done.7
  109.6 0.1 add_convert_fusion.7
  109.7 0.6 collective-permute-start.13
  110.3 4.1 %collective-permute-done.19 = bf16[2,2,256,128]{3,2,1,0:T(8,128)(2,1)S(1)} collective-permute-done((bf16[2,2,256,128]{3,2,1,0:T(8,128)(2,1)S(1)}, bf16[2,2,256,128]{3,2,1,0:T(8,128)(2,1)S(1)}, u32[]{:S(2)}, u32[]{:S(2)}) %collective-permute-start.19) | collective-permute-done | bytes 262176 | tf_op jit(solution)/shard_map/ppermute | solution.py:21
  114.5 0.7 fusion.12
  115.2 4.9 %collective-permute-done.17 = bf16[2,2,256,128]{3,2,1,0:T(8,128)(2,1)S(1)} collective-permute-done((bf16[2,2,256,128]{3,2,1,0:T(8,128)(2,1)S(1)}, bf16[2,2,256,128]{3,2,1,0:T(8,128)(2,1)S(1)}, u32[]{:S(2)}, u32[]{:S(2)}) %collective-permute-start.17) | collective-permute-done | bytes 262176 | tf_op jit(solution)/shard_map/ppermute | solution.py:21
  120.2 5.6 %collective-permute-done.15 = bf16[2,2,256,128]{3,2,1,0:T(8,128)(2,1)S(1)} collective-permute-done((bf16[2,2,256,128]{3,2,1,0:T(8,128)(2,1)S(1)}, bf16[2,2,256,128]{3,2,1,0:T(8,128)(2,1)S(1)}, u32[]{:S(2)}, u32[]{:S(2)}) %collective-permute-start.15) | collective-permute-done | bytes 262176 | tf_op jit(solution)/shard_map/ppermute | solution.py:21
  125.8 0.7 fusion.11
  126.4 0.7 fusion.10
  127.1 4.2 %collective-permute-done.13 = bf16[2,2,256,128]{3,2,1,0:T(8,128)(2,1)S(1)} collective-permute-done((bf16[2,2,256,128]{3,2,1,0:T(8,128)(2,1)S(1)}, bf16[2,2,256,128]{3,2,1,0:T(8,128)(2,1)S(1)}, u32[]{:S(2)}, u32[]{:S(2)}) %collective-permute-start.13) | collective-permute-done | bytes 262176 | tf_op jit(solution)/shard_map/ppermute | solution.py:21
  131.4 0.7 fusion.9
  132.1 0.1 pad_maximum_fusion.1
  132.1 1.0 collective-permute-start.20
  133.1 0.8 slice_bitcast_fusion.8
  133.9 2.5 %unpack.2 = (bf16[256,1024]{1,0:T(8,128)(2,1)}, bf16[256,1024]{1,0:T(8,128)(2,1)}) custom-call(s32[1]{0:T(128)} %bitcast.core_ref, bf16[2,256,128]{2,1,0:T(8,128)(2,1)} %get-tuple-element.41.refs_0_, bf16[2,256,128]{2,1,0:T(8,128)(2,1)} %get-tuple-element.43.refs_1_, bf16[2,256,128]{2,1,0:T(8,128)(2,1)} %get-tuple-element.45.refs_2_, ...), custom_call_target="tpu_custom_call" | custom-call | tf_op jit(solution)/shard_map/unpack/pallas_call | solution.py:100
  136.4 0.8 slice_bitcast_fusion
  137.3 2.5 %unpack.3 = (bf16[256,1024]{1,0:T(8,128)(2,1)}, bf16[256,1024]{1,0:T(8,128)(2,1)}) custom-call(s32[1]{0:T(128)} %bitcast.core_ref, bf16[2,256,128]{2,1,0:T(8,128)(2,1)} %get-tuple-element.77.refs_0_, bf16[2,256,128]{2,1,0:T(8,128)(2,1)} %get-tuple-element.79.refs_1_, bf16[2,256,128]{2,1,0:T(8,128)(2,1)} %get-tuple-element.81.refs_2_, ...), custom_call_target="tpu_custom_call" | custom-call | tf_op jit(solution)/shard_map/unpack/pallas_call | solution.py:100
  (61 shorter events, 0.4 us)
Async XLA Ops:
  3.1 2.1 %collective-permute-start.2 = (bf16[4,2,256,128]{3,2,1,0:T(8,128)(2,1)}, bf16[4,2,256,128]{3,2,1,0:T(8,128)(2,1)S(1)}, u32[]{:S(2)}, u32[]{:S(2)}) collective-permute-start(bf16[4,2,256,128]{3,2,1,0:T(8,128)(2,1)} %get-tuple-element.39), channel_id=1, source_target_pairs={{0,1},{1,0},{2,3},{3,2},{4,5},{5,4},{6,7},{7,6},{8,9},{9,8},{10,11... | collective-permute-start | bytes 1572872 | tf_op jit(solution)/shard_map/ppermute | solution.py:21
  5.2 0.8 copy-start.8
  8.2 6.9 %copy-start.16 = (bf16[2,2,256,128]{3,2,1,0:T(8,128)(2,1)S(1)}, bf16[2,2,256,128]{3,2,1,0:T(8,128)(2,1)}, u32[]{:S(2)}) copy-start(bf16[2,2,256,128]{3,2,1,0:T(8,128)(2,1)} %get-tuple-element.44.kv_own) | copy-start | bytes 786436
  8.2 7.8 %copy-start.15 = (bf16[2,2,256,128]{3,2,1,0:T(8,128)(2,1)S(1)}, bf16[2,2,256,128]{3,2,1,0:T(8,128)(2,1)}, u32[]{:S(2)}) copy-start(bf16[2,2,256,128]{3,2,1,0:T(8,128)(2,1)} %get-tuple-element.42.kv_own) | copy-start | bytes 786436
  8.2 8.5 %copy-start.14 = (bf16[2,2,256,128]{3,2,1,0:T(8,128)(2,1)S(1)}, bf16[2,2,256,128]{3,2,1,0:T(8,128)(2,1)}, u32[]{:S(2)}) copy-start(bf16[2,2,256,128]{3,2,1,0:T(8,128)(2,1)} %get-tuple-element.40.kv_own) | copy-start | bytes 786436
  8.2 9.3 %collective-permute-start.9 = (bf16[2,2,256,128]{3,2,1,0:T(8,128)(2,1)}, bf16[2,2,256,128]{3,2,1,0:T(8,128)(2,1)S(1)}, u32[]{:S(2)}, u32[]{:S(2)}) collective-permute-start(bf16[2,2,256,128]{3,2,1,0:T(8,128)(2,1)} %get-tuple-element.46.kv_own), channel_id=1, source_target_pairs={{0,2},{1,3},{2,0},{3,1},{4,6},{5,7},{6,4},{7,5},{8,10},{9,11},{10,... | collective-permute-start | bytes 786440 | tf_op jit(solution)/shard_map/ppermute | solution.py:21
  13.0 0.7 copy-start.25
  13.0 22.6 %collective-permute-start.1 = (bf16[4,2,256,128]{3,2,1,0:T(8,128)(2,1)}, bf16[4,2,256,128]{3,2,1,0:T(8,128)(2,1)S(1)}, u32[]{:S(2)}, u32[]{:S(2)}) collective-permute-start(bf16[4,2,256,128]{3,2,1,0:T(8,128)(2,1)} %get-tuple-element.37), channel_id=1, source_target_pairs={{0,1},{1,0},{2,3},{3,2},{4,5},{5,4},{6,7},{7,6},{8,9},{9,8},{10,11... | collective-permute-start | bytes 1572872 | tf_op jit(solution)/shard_map/ppermute | solution.py:21
  13.7 0.7 copy-start.12
  14.5 1.5 %collective-permute-start = (s32[2,9]{1,0:T(2,128)S(1)}, s32[2,9]{1,0:T(2,128)S(1)}, u32[]{:S(2)}, u32[]{:S(2)}) collective-permute-start(s32[2,9]{1,0:T(2,128)S(1)} %pad_add_fusion.1), channel_id=1, source_target_pairs={{0,1},{1,0},{2,3},{3,2},{4,5},{5,4},{6,7},{7,6},{8,9},{9,8},{10,11... | collective-permute-start | bytes 224 | tf_op jit(solution)/shard_map/ppermute | solution.py:21
  15.1 7.8 %collective-permute-start.7 = (bf16[2,2,256,128]{3,2,1,0:T(8,128)(2,1)S(1)}, bf16[2,2,256,128]{3,2,1,0:T(8,128)(2,1)S(1)}, u32[]{:S(2)}, u32[]{:S(2)}) collective-permute-start(bf16[2,2,256,128]{3,2,1,0:T(8,128)(2,1)S(1)} %copy-done.16), channel_id=1, source_target_pairs={{0,2},{1,3},{2,0},{3,1},{4,6},{5,7},{6,4},{7,5},{8,10},{9,11},{10,... | collective-permute-start | bytes 786440 | tf_op jit(solution)/shard_map/ppermute | solution.py:21
  16.0 12.5 %collective-permute-start.5 = (bf16[2,2,256,128]{3,2,1,0:T(8,128)(2,1)S(1)}, bf16[2,2,256,128]{3,2,1,0:T(8,128)(2,1)S(1)}, u32[]{:S(2)}, u32[]{:S(2)}) collective-permute-start(bf16[2,2,256,128]{3,2,1,0:T(8,128)(2,1)S(1)} %copy-done.15), channel_id=1, source_target_pairs={{0,2},{1,3},{2,0},{3,1},{4,6},{5,7},{6,4},{7,5},{8,10},{9,11},{10,... | collective-permute-start | bytes 786440 | tf_op jit(solution)/shard_map/ppermute | solution.py:21
  16.7 17.5 %collective-permute-start.3 = (bf16[2,2,256,128]{3,2,1,0:T(8,128)(2,1)S(1)}, bf16[2,2,256,128]{3,2,1,0:T(8,128)(2,1)S(1)}, u32[]{:S(2)}, u32[]{:S(2)}) collective-permute-start(bf16[2,2,256,128]{3,2,1,0:T(8,128)(2,1)S(1)} %copy-done.14), channel_id=1, source_target_pairs={{0,2},{1,3},{2,0},{3,1},{4,6},{5,7},{6,4},{7,5},{8,10},{9,11},{10,... | collective-permute-start | bytes 786440 | tf_op jit(solution)/shard_map/ppermute | solution.py:21
  17.5 18.2 %copy-start.17 = (bf16[2,2,256,128]{3,2,1,0:T(8,128)(2,1)}, bf16[2,2,256,128]{3,2,1,0:T(8,128)(2,1)S(1)}, u32[]{:S(2)}) copy-start(bf16[2,2,256,128]{3,2,1,0:T(8,128)(2,1)S(1)} %collective-permute-done.9.kv_pair) | copy-start | bytes 786436
  17.5 18.2 %collective-permute-start.10 = (bf16[2,2,256,128]{3,2,1,0:T(8,128)(2,1)S(1)}, bf16[2,2,256,128]{3,2,1,0:T(8,128)(2,1)S(1)}, u32[]{:S(2)}, u32[]{:S(2)}) collective-permute-start(bf16[2,2,256,128]{3,2,1,0:T(8,128)(2,1)S(1)} %collective-permute-done.9.kv_pair), channel_id=1, source_target_pairs={{0,4},{1,5},{2,14},{3,15},{4,8},{5,9},{6,2},{7,3},{8,12},{9,13},{1... | collective-permute-start | bytes 786440 | tf_op jit(solution)/shard_map/ppermute | solution.py:21
  22.9 27.0 %copy-start.20 = (bf16[2,2,256,128]{3,2,1,0:T(8,128)(2,1)}, bf16[2,2,256,128]{3,2,1,0:T(8,128)(2,1)S(1)}, u32[]{:S(2)}) copy-start(bf16[2,2,256,128]{3,2,1,0:T(8,128)(2,1)S(1)} %collective-permute-done.7.kv_pair) | copy-start | bytes 786436
  22.9 31.4 %collective-permute-start.8 = (bf16[2,2,256,128]{3,2,1,0:T(8,128)(2,1)S(1)}, bf16[2,2,256,128]{3,2,1,0:T(8,128)(2,1)S(1)}, u32[]{:S(2)}, u32[]{:S(2)}) collective-permute-start(bf16[2,2,256,128]{3,2,1,0:T(8,128)(2,1)S(1)} %collective-permute-done.7.kv_pair), channel_id=1, source_target_pairs={{0,4},{1,5},{2,14},{3,15},{4,8},{5,9},{6,2},{7,3},{8,12},{9,13},{1... | collective-permute-start | bytes 786440 | tf_op jit(solution)/shard_map/ppermute | solution.py:21
  28.5 21.4 %copy-start.19 = (bf16[2,2,256,128]{3,2,1,0:T(8,128)(2,1)}, bf16[2,2,256,128]{3,2,1,0:T(8,128)(2,1)S(1)}, u32[]{:S(2)}) copy-start(bf16[2,2,256,128]{3,2,1,0:T(8,128)(2,1)S(1)} %collective-permute-done.5.kv_pair) | copy-start | bytes 786436
  28.6 42.3 %collective-permute-start.6 = (bf16[2,2,256,128]{3,2,1,0:T(8,128)(2,1)S(1)}, bf16[2,2,256,128]{3,2,1,0:T(8,128)(2,1)S(1)}, u32[]{:S(2)}, u32[]{:S(2)}) collective-permute-start(bf16[2,2,256,128]{3,2,1,0:T(8,128)(2,1)S(1)} %collective-permute-done.5.kv_pair), channel_id=1, source_target_pairs={{0,4},{1,5},{2,14},{3,15},{4,8},{5,9},{6,2},{7,3},{8,12},{9,13},{1... | collective-permute-start | bytes 786440 | tf_op jit(solution)/shard_map/ppermute | solution.py:21
  34.2 15.7 %copy-start.18 = (bf16[2,2,256,128]{3,2,1,0:T(8,128)(2,1)}, bf16[2,2,256,128]{3,2,1,0:T(8,128)(2,1)S(1)}, u32[]{:S(2)}) copy-start(bf16[2,2,256,128]{3,2,1,0:T(8,128)(2,1)S(1)} %collective-permute-done.3.kv_pair) | copy-start | bytes 786436
  34.2 53.4 %collective-permute-start.4 = (bf16[2,2,256,128]{3,2,1,0:T(8,128)(2,1)S(1)}, bf16[2,2,256,128]{3,2,1,0:T(8,128)(2,1)S(1)}, u32[]{:S(2)}, u32[]{:S(2)}) collective-permute-start(bf16[2,2,256,128]{3,2,1,0:T(8,128)(2,1)S(1)} %collective-permute-done.3.kv_pair), channel_id=1, source_target_pairs={{0,4},{1,5},{2,14},{3,15},{4,8},{5,9},{6,2},{7,3},{8,12},{9,13},{1... | collective-permute-start | bytes 786440 | tf_op jit(solution)/shard_map/ppermute | solution.py:21
  35.6 0.8 copy-start.13
  35.6 0.9 copy-start.24
  49.9 56.6 %collective-permute-start.18 = (bf16[2,2,256,128]{3,2,1,0:T(8,128)(2,1)}, bf16[2,2,256,128]{3,2,1,0:T(8,128)(2,1)S(1)}, u32[]{:S(2)}, u32[]{:S(2)}) collective-permute-start(bf16[2,2,256,128]{3,2,1,0:T(8,128)(2,1)} %get-tuple-element.65), channel_id=1, source_target_pairs={{0,12},{1,13},{2,6},{3,7},{4,0},{5,1},{6,10},{7,11},{8,4},{9,5},{1... | collective-permute-start | bytes 786440 | tf_op jit(solution)/shard_map/ppermute | solution.py:21
  54.3 0.7 copy-start.23
  68.6 38.1 %collective-permute-start.16 = (bf16[2,2,256,128]{3,2,1,0:T(8,128)(2,1)}, bf16[2,2,256,128]{3,2,1,0:T(8,128)(2,1)S(1)}, u32[]{:S(2)}, u32[]{:S(2)}) collective-permute-start(bf16[2,2,256,128]{3,2,1,0:T(8,128)(2,1)} %get-tuple-element.62), channel_id=1, source_target_pairs={{0,12},{1,13},{2,6},{3,7},{4,0},{5,1},{6,10},{7,11},{8,4},{9,5},{1... | collective-permute-start | bytes 786440 | tf_op jit(solution)/shard_map/ppermute | solution.py:21
  70.9 0.7 copy-start.22
  85.2 18.7 %copy-start.9 = (bf16[2,256,128]{2,1,0:T(8,128)(2,1)S(1)}, bf16[2,256,128]{2,1,0:T(8,128)(2,1)}, u32[]{:S(2)}) copy-start(bf16[2,256,128]{2,1,0:T(8,128)(2,1)} %get-tuple-element.51) | copy-start | bytes 393220
  85.2 18.7 %copy-start.10 = (bf16[2,256,128]{2,1,0:T(8,128)(2,1)S(1)}, bf16[2,256,128]{2,1,0:T(8,128)(2,1)}, u32[]{:S(2)}) copy-start(bf16[2,256,128]{2,1,0:T(8,128)(2,1)} %get-tuple-element.50) | copy-start | bytes 393220
  85.2 18.7 %copy-start.11 = (bf16[2,256,128]{2,1,0:T(8,128)(2,1)S(1)}, bf16[2,256,128]{2,1,0:T(8,128)(2,1)}, u32[]{:S(2)}) copy-start(bf16[2,256,128]{2,1,0:T(8,128)(2,1)} %get-tuple-element.49) | copy-start | bytes 393220
  85.2 23.1 %collective-permute-start.14 = (bf16[2,2,256,128]{3,2,1,0:T(8,128)(2,1)}, bf16[2,2,256,128]{3,2,1,0:T(8,128)(2,1)S(1)}, u32[]{:S(2)}, u32[]{:S(2)}) collective-permute-start(bf16[2,2,256,128]{3,2,1,0:T(8,128)(2,1)} %get-tuple-element.59), channel_id=1, source_target_pairs={{0,12},{1,13},{2,6},{3,7},{4,0},{5,1},{6,10},{7,11},{8,4},{9,5},{1... | collective-permute-start | bytes 786440 | tf_op jit(solution)/shard_map/ppermute | solution.py:21
  87.5 0.7 copy-start.21
  101.6 7.7 %collective-permute-start.12 = (bf16[2,2,256,128]{3,2,1,0:T(8,128)(2,1)}, bf16[2,2,256,128]{3,2,1,0:T(8,128)(2,1)S(1)}, u32[]{:S(2)}, u32[]{:S(2)}) collective-permute-start(bf16[2,2,256,128]{3,2,1,0:T(8,128)(2,1)} %get-tuple-element.56), channel_id=1, source_target_pairs={{0,12},{1,13},{2,6},{3,7},{4,0},{5,1},{6,10},{7,11},{8,4},{9,5},{1... | collective-permute-start | bytes 786440 | tf_op jit(solution)/shard_map/ppermute | solution.py:21
  103.9 2.6 %copy-start.4 = (f32[2,2,256,128]{3,2,1,0:T(8,128)S(1)}, f32[2,2,256,128]{3,2,1,0:T(8,128)}, u32[]{:S(2)}) copy-start(f32[2,2,256,128]{3,2,1,0:T(8,128)} %get-tuple-element.64) | copy-start | bytes 1572868
  104.9 28.2 %collective-permute-start.11 = (bf16[4,2,256,128]{3,2,1,0:T(8,128)(2,1)S(1)}, bf16[4,2,256,128]{3,2,1,0:T(8,128)(2,1)S(1)}, u32[]{:S(2)}, u32[]{:S(2)}) collective-permute-start(bf16[4,2,256,128]{3,2,1,0:T(8,128)(2,1)S(1)} %pad_maximum_fusion), channel_id=1, source_target_pairs={{0,1},{1,0},{2,3},{3,2},{4,5},{5,4},{6,7},{7,6},{8,9},{9,8},{10,11... | collective-permute-start | bytes 1572872 | tf_op jit(solution)/shard_map/ppermute | solution.py:21
  106.5 1.0 copy-start.5
  106.6 7.9 %collective-permute-start.19 = (bf16[2,2,256,128]{3,2,1,0:T(8,128)(2,1)S(1)}, bf16[2,2,256,128]{3,2,1,0:T(8,128)(2,1)S(1)}, u32[]{:S(2)}, u32[]{:S(2)}) collective-permute-start(bf16[2,2,256,128]{3,2,1,0:T(8,128)(2,1)S(1)} %add_convert_fusion.1), channel_id=1, source_target_pairs={{0,2},{1,3},{2,0},{3,1},{4,6},{5,7},{6,4},{7,5},{8,10},{9,11},{10,... | collective-permute-start | bytes 786440 | tf_op jit(solution)/shard_map/ppermute | solution.py:21
  107.6 1.0 copy-start.6
  107.6 12.5 %collective-permute-start.17 = (bf16[2,2,256,128]{3,2,1,0:T(8,128)(2,1)S(1)}, bf16[2,2,256,128]{3,2,1,0:T(8,128)(2,1)S(1)}, u32[]{:S(2)}, u32[]{:S(2)}) collective-permute-start(bf16[2,2,256,128]{3,2,1,0:T(8,128)(2,1)S(1)} %add_convert_fusion.3), channel_id=1, source_target_pairs={{0,2},{1,3},{2,0},{3,1},{4,6},{5,7},{6,4},{7,5},{8,10},{9,11},{10,... | collective-permute-start | bytes 786440 | tf_op jit(solution)/shard_map/ppermute | solution.py:21
  108.6 1.0 copy-start.7
  108.7 17.0 %collective-permute-start.15 = (bf16[2,2,256,128]{3,2,1,0:T(8,128)(2,1)S(1)}, bf16[2,2,256,128]{3,2,1,0:T(8,128)(2,1)S(1)}, u32[]{:S(2)}, u32[]{:S(2)}) collective-permute-start(bf16[2,2,256,128]{3,2,1,0:T(8,128)(2,1)S(1)} %add_convert_fusion.5), channel_id=1, source_target_pairs={{0,2},{1,3},{2,0},{3,1},{4,6},{5,7},{6,4},{7,5},{8,10},{9,11},{10,... | collective-permute-start | bytes 786440 | tf_op jit(solution)/shard_map/ppermute | solution.py:21
  109.6 4.8 %copy-start = (f32[2,2,256,128]{3,2,1,0:T(8,128)S(1)}, f32[2,2,256,128]{3,2,1,0:T(8,128)}, u32[]{:S(2)}) copy-start(f32[2,2,256,128]{3,2,1,0:T(8,128)} %get-tuple-element.63) | copy-start | bytes 1572868
  109.7 21.6 %collective-permute-start.13 = (bf16[2,2,256,128]{3,2,1,0:T(8,128)(2,1)S(1)}, bf16[2,2,256,128]{3,2,1,0:T(8,128)(2,1)S(1)}, u32[]{:S(2)}, u32[]{:S(2)}) collective-permute-start(bf16[2,2,256,128]{3,2,1,0:T(8,128)(2,1)S(1)} %add_convert_fusion.7), channel_id=1, source_target_pairs={{0,2},{1,3},{2,0},{3,1},{4,6},{5,7},{6,4},{7,5},{8,10},{9,11},{10,... | collective-permute-start | bytes 786440 | tf_op jit(solution)/shard_map/ppermute | solution.py:21
  114.5 5.6 %copy-start.1 = (f32[2,2,256,128]{3,2,1,0:T(8,128)S(1)}, f32[2,2,256,128]{3,2,1,0:T(8,128)}, u32[]{:S(2)}) copy-start(f32[2,2,256,128]{3,2,1,0:T(8,128)} %get-tuple-element.60) | copy-start | bytes 1572868
  120.1 5.6 %copy-start.2 = (f32[2,2,256,128]{3,2,1,0:T(8,128)S(1)}, f32[2,2,256,128]{3,2,1,0:T(8,128)}, u32[]{:S(2)}) copy-start(f32[2,2,256,128]{3,2,1,0:T(8,128)} %get-tuple-element.57) | copy-start | bytes 1572868
  125.8 5.6 %copy-start.3 = (f32[2,2,256,128]{3,2,1,0:T(8,128)S(1)}, f32[2,2,256,128]{3,2,1,0:T(8,128)}, u32[]{:S(2)}) copy-start(f32[2,2,256,128]{3,2,1,0:T(8,128)} %get-tuple-element.54) | copy-start | bytes 1572868
  132.1 4.3 %collective-permute-start.20 = (bf16[4,2,256,128]{3,2,1,0:T(8,128)(2,1)S(1)}, bf16[4,2,256,128]{3,2,1,0:T(8,128)(2,1)S(1)}, u32[]{:S(2)}, u32[]{:S(2)}) collective-permute-start(bf16[4,2,256,128]{3,2,1,0:T(8,128)(2,1)S(1)} %pad_maximum_fusion.1), channel_id=1, source_target_pairs={{0,1},{1,0},{2,3},{3,2},{4,5},{5,4},{6,7},{7,6},{8,9},{9,8},{10,11... | collective-permute-start | bytes 1572872 | tf_op jit(solution)/shard_map/ppermute | solution.py:21

commit v2 on v1

v2 whole, which is shorter than its diff:
```python
import functools
import math

import jax
import jax.numpy as jnp
from jax import lax
from jax.experimental import pallas as pl
from jax.experimental.pallas import tpu as pltpu
from jax.sharding import PartitionSpec as P


LANES = 128
F32 = jnp.float32
BF16 = jnp.bfloat16
VMEM = pl.BlockSpec(memory_space=pltpu.VMEM)
SMEM = pl.BlockSpec(memory_space=pltpu.SMEM)
ANY = pl.BlockSpec(memory_space=pl.ANY)


def permuted(x, target):
    length = lax.axis_size("blk")
    return lax.ppermute(x, "blk", [(i, target(i) % length) for i in range(length)])


def core_swap(x):
    return permuted(x, lambda i: i ^ 1)


def pair_swap(x):
    return permuted(x, lambda i: i ^ 2)


def cross_swap(x):
    return permuted(x, lambda i: i ^ 3)


def relay(x, sign):
    return permuted(x, lambda i: i + sign * 4 if (i & 2) == 0 else i - sign * 4)


def dot(a, b):
    return jnp.dot(a, b, preferred_element_type=F32)


def columns(core, half, chunk, lanes):
    mine = pl.multiple_of(core * half + chunk * lanes, lanes)
    other = pl.multiple_of((1 - core) * half + chunk * lanes, lanes)
    return pl.ds(mine, lanes), pl.ds(other, lanes)


def run_copies(copies, sems):
    started = [
        pltpu.make_async_copy(source, target, sems.at[i])
        for i, (source, target) in enumerate(copies)
    ]
    for copy in started:
        copy.start()
    for copy in started:
        copy.wait()


def small(limit=4):
    return pltpu.CompilerParams(vmem_limit_bytes=limit << 20)


def pack_body(first, core_ref, a_ref, b_ref, keep_ref, send_ref, sems):
    copies = []
    for index, ref in enumerate((a_ref, b_ref)):
        for chunk in range(keep_ref.shape[0]):
            mine, other = columns(core_ref[0], ref.shape[1] // 2, first + chunk, LANES)
            copies.append((ref.at[:, mine], keep_ref.at[chunk, index]))
            copies.append((ref.at[:, other], send_ref.at[chunk, index]))
    run_copies(copies, sems)


def pack(core, a, b, first, last):
    rows = a.shape[0]
    shape = jax.ShapeDtypeStruct((last - first, 2, rows, LANES), a.dtype)
    return pl.pallas_call(
        functools.partial(pack_body, first),
        out_shape=(shape, shape),
        in_specs=[SMEM, ANY, ANY],
        out_specs=(VMEM, VMEM),
        scratch_shapes=[pltpu.SemaphoreType.DMA((4 * (last - first),))],
        compiler_params=small(),
        name="pack",
    )(
        core,
        pltpu.with_memory_space_constraint(a, pltpu.HBM),
        pltpu.with_memory_space_constraint(b, pltpu.HBM),
    )


def zip_body(keep_ref, recv_ref, *out_refs):
    for chunk, out_ref in enumerate(out_refs):
        out_ref[0] = keep_ref[chunk]
        out_ref[1] = recv_ref[chunk]


def zip_chunks(keep, recv):
    shape = jax.ShapeDtypeStruct((2,) + keep.shape[1:], keep.dtype)
    return pl.pallas_call(
        zip_body,
        out_shape=(shape,) * keep.shape[0],
        in_specs=[VMEM, VMEM],
        out_specs=(VMEM,) * keep.shape[0],
        compiler_params=small(),
        name="zip",
    )(keep, recv)


def place_body(count, first, aliased, core_ref, *refs):
    a_ref, b_ref, stage, sems = refs[-4:]
    copies = []
    for c in range(count):
        mine, other = columns(core_ref[0], a_ref.shape[1] // 2, first + c, LANES)
        for index, ref in enumerate((a_ref, b_ref)):
            if len(refs) - 4 - aliased == 2 * count:
                copies.append((refs[c].at[index], ref.at[:, mine]))
                copies.append((refs[count + c].at[index], ref.at[:, other]))
            else:
                own, own_add, cross, cross_add = refs[4 * c : 4 * c + 4]
                stage[c, 0, index] = (own[index] + own_add[index].astype(F32)).astype(BF16)
                total = cross[2 + index].astype(F32) + cross_add[index].astype(F32)
                stage[c, 1, index] = total.astype(BF16)
                copies.append((stage.at[c, 0, index], ref.at[:, mine]))
                copies.append((stage.at[c, 1, index], ref.at[:, other]))
    run_copies(copies, sems)


def place(core, pieces, count, first, width, onto=()):
    rows = pieces[0].shape[1]
    shape = jax.ShapeDtypeStruct((rows, width), BF16)
    aliases = {1 + len(pieces) + i: i for i in range(len(onto))}
    return pl.pallas_call(
        functools.partial(place_body, count, first, len(onto)),
        out_shape=(shape, shape),
        in_specs=[SMEM] + [VMEM] * len(pieces) + [ANY] * len(onto),
        out_specs=(ANY, ANY),
        scratch_shapes=[
            pltpu.VMEM((count, 2, 2, rows, LANES), BF16),
            pltpu.SemaphoreType.DMA((4 * count,)),
        ],
        input_output_aliases=aliases,
        compiler_params=small(8),
        name="place",
    )(core, *pieces, *onto)


def attend_body(
    slots,
    counts,
    qg_keep,
    qg_recv,
    *refs,
):
    kv_refs, refs = refs[:-19], refs[-19:]
    od_keep, to_partner, g_mine, g_pair, g_far = refs[:5]
    kw, vw, kt, vt, dk, dv, far, scores, expd, dscores, qd, gd, in_sems, out_sems = refs[5:]
    kv_at = []
    for ref in kv_refs:
        kv_at += [ref] if len(ref.shape) == 4 else [ref.at[0], ref.at[1]]
    blk = kw.shape[1]
    own_blocks = kv_at[0].shape[1]
    chip_blocks = 2 * own_blocks
    list_width = slots.shape[0] // chip_blocks
    head_dim = LANES // 2
    factor = 1.0 / math.sqrt(head_dim)
    places = [(buf, src) for buf in range(3) for src in range(2)]
    loads = []
    for buf, src in places:
        spot = pl.ds((buf * 2 + src) * own_blocks, own_blocks)
        for kind, window in enumerate((kw, vw)):
            loads.append(
                pltpu.make_async_copy(
                    kv_at[buf * 2 + src].at[kind],
                    window.at[spot],
                    in_sems.at[len(loads)],
                )
            )
    for load in loads:
        load.start()
    dk[...] = jnp.zeros_like(dk)
    dv[...] = jnp.zeros_like(dv)
    row_ids = lax.broadcasted_iota(jnp.int32, (LANES, blk), 0)
    first_rows = row_ids < head_dim
    first_lanes = lax.broadcasted_iota(jnp.int32, (blk, LANES), 1) < head_dim

    def diagonal_t(tile_t):
        zero = jnp.zeros_like(tile_t)
        return jnp.concatenate(
            [jnp.where(first_rows, tile_t, zero), jnp.where(first_rows, zero, tile_t)], axis=1
        )

    def collapse(wide):
        return jnp.where(first_rows, wide[:, :blk], wide[:, blk:])

    def slot(unit, s):
        return slots[unit * list_width + s]

    def gathered(window, unit, axis):
        return jnp.concatenate([window[slot(unit, s)] for s in range(list_width)], axis=axis)

    def live(unit, s):
        return s < counts[unit]

    def fold(tile, op):
        return op(tile.reshape(tile.shape[0] // 8, 8, tile.shape[1]), axis=0)

    def score_phase(unit):
        src, b = divmod(unit, own_blocks)
        rows = slice(b * blk, (b + 1) * blk)
        source = (qg_keep, qg_recv)[src]
        q_tile = source[0, 0, rows, :].astype(F32) * factor
        g_tile = source[0, 1, rows, :].astype(F32)
        q_diag = diagonal_t(q_tile.T).astype(BF16)
        qd[unit % 2] = q_diag
        gd[unit % 2] = diagonal_t(g_tile.T).astype(BF16)
        wide = dot(gathered(kw, unit, 0), q_diag)
        best = None
        for s in range(list_width):
            tile = wide[s * blk : (s + 1) * blk]
            scores[unit % 2, s] = tile
            top = fold(tile, jnp.max)
            if s >= 2:
                top = jnp.where(live(unit, s), top, -jnp.inf)
            best = top if best is None else jnp.maximum(best, top)
        return jnp.max(best, axis=0, keepdims=True)

    def value_phase(unit, row_max):
        total = None
        for s in range(list_width):
            base = row_max
            if s >= 2:
                base = jnp.where(live(unit, s), row_max, jnp.inf)
            e = jnp.exp(scores[unit % 2, s] - base)
            sums = fold(e, jnp.sum)
            total = sums if total is None else total + sums
            expd[unit % 2, s * blk : (s + 1) * blk] = e.astype(BF16)
        mixed = dot(gathered(vt, unit, 1), expd[unit % 2])
        return mixed, 1.0 / jnp.sum(total, axis=0, keepdims=True)

    def grad_phase(unit, mixed, inverse):
        q_t = qd[unit % 2].astype(F32)
        g_t = gd[unit % 2].astype(F32)
        src, b = divmod(unit, own_blocks)
        rows = slice(b * blk, (b + 1) * blk)
        out_ref = (od_keep, to_partner)[src]
        out_t = mixed * inverse
        out_ref[0, rows, :] = collapse(out_t).T.astype(BF16)
        delta = jnp.sum(g_t * out_t.astype(BF16).astype(F32), axis=0, keepdims=True)
        g_bf = (g_t * inverse).T.astype(BF16)
        q_bf = (q_t * inverse).T.astype(BF16)
        dp = dot(gathered(vw, unit, 0), gd[unit % 2])
        for s in range(list_width):
            part = slice(s * blk, (s + 1) * blk)
            e = expd[unit % 2, part].astype(F32)
            dscores[unit % 2, part] = (e * (dp[part] - delta)).astype(BF16)
        moved = dot(gathered(kt, unit, 1), dscores[unit % 2])
        dv_all = dot(expd[unit % 2], g_bf)
        for s in range(list_width):
            dv[slot(unit, s)] += dv_all[s * blk : (s + 1) * blk]
        dk_all = dot(dscores[unit % 2], q_bf)
        for s in range(list_width):
            dk[slot(unit, s)] += dk_all[s * blk : (s + 1) * blk]
        out_ref[1, rows, :] = (collapse(moved * inverse) * factor).T.astype(BF16)

    for load in loads:
        load.wait()
    for index in range(3 * chip_blocks):
        kt[index] = kw[index].T
        vt[index] = vw[index].T
    ahead = score_phase(0)
    for unit in range(chip_blocks):
        row_max = ahead
        mixed, inverse = value_phase(unit, row_max)
        if unit + 1 < chip_blocks:
            ahead = score_phase(unit + 1)
        grad_phase(unit, mixed, inverse)

    stores = []

    def store(source, target):
        stores.append(pltpu.make_async_copy(source, target, out_sems.at[len(stores)]))
        stores[-1].start()

    for buf, src in reversed(places):
        spot = pl.ds((buf * 2 + src) * own_blocks, own_blocks)
        for kind, window in enumerate((dk, dv)):
            if buf == 2:
                far[src, kind] = window[spot].astype(BF16)
                store(far.at[src, kind], g_far.at[src, kind])
            elif buf == 1:
                store(window.at[spot], g_pair.at[src, kind])
            elif src == 0:
                store(window.at[spot], g_mine.at[kind])
            else:
                to_partner[2 + kind] = window[spot].reshape(to_partner.shape[1:]).astype(BF16)
    for copy in stores:
        copy.wait()


def attend(chunk, slots, counts, qg_keep, qg_recv, kv, blk):
    rows = qg_keep.shape[2]
    own_blocks = rows // blk
    chip_blocks = 2 * own_blocks
    window = 3 * chip_blocks
    list_width = slots.shape[0] // chip_blocks
    column = pl.BlockSpec((1, 2, rows, LANES), lambda i: (chunk, 0, 0, 0))
    units = chip_blocks * list_width
    tail = (own_blocks, blk, LANES)
    kv = [x.reshape(x.shape[:-2] + tail) for x in kv]
    outs = pl.pallas_call(
        attend_body,
        grid=(1,),
        out_shape=(
            jax.ShapeDtypeStruct((2, rows, LANES), BF16),
            jax.ShapeDtypeStruct((4, rows, LANES), BF16),
            jax.ShapeDtypeStruct((2,) + tail, F32),
            jax.ShapeDtypeStruct((2, 2) + tail, F32),
            jax.ShapeDtypeStruct((2, 2) + tail, BF16),
        ),
        in_specs=[SMEM, SMEM, column, column] + [ANY] * len(kv),
        out_specs=(
            pl.BlockSpec((2, rows, LANES), lambda i: (0, 0, 0)),
            pl.BlockSpec((4, rows, LANES), lambda i: (0, 0, 0)),
            ANY,
            ANY,
            ANY,
        ),
        scratch_shapes=[
            pltpu.VMEM((window, blk, LANES), BF16),
            pltpu.VMEM((window, blk, LANES), BF16),
            pltpu.VMEM((window, LANES, blk), BF16),
            pltpu.VMEM((window, LANES, blk), BF16),
            pltpu.VMEM((window, blk, LANES), F32),
            pltpu.VMEM((window, blk, LANES), F32),
            pltpu.VMEM((2, 2) + tail, BF16),
            pltpu.VMEM((2, list_width, blk, 2 * blk), F32),
            pltpu.VMEM((2, list_width * blk, 2 * blk), BF16),
            pltpu.VMEM((2, list_width * blk, 2 * blk), BF16),
            pltpu.VMEM((2, LANES, 2 * blk), BF16),
            pltpu.VMEM((2, LANES, 2 * blk), BF16),
            pltpu.SemaphoreType.DMA((12,)),
            pltpu.SemaphoreType.DMA((10,)),
        ],
        compiler_params=pltpu.CompilerParams(vmem_limit_bytes=24 << 20),
        cost_estimate=pl.CostEstimate(
            flops=units * 24 * blk * blk * LANES,
            transcendentals=units * 2 * blk * blk,
            bytes_accessed=16 * rows * LANES * 4,
        ),
        name="attend",
    )(slots, counts, qg_keep, qg_recv, *kv)
    return tuple(x.reshape(x.shape[:-3] + (rows, LANES)) if x.ndim > 3 else x for x in outs)


def local(query, key_in, value, grad_out, neighbors, counts):
    rows, width = query.shape
    own_blocks, list_width = neighbors.shape
    blk = rows // own_blocks
    chunks = width // 2 // LANES
    shard_count = lax.axis_size("blk")
    shard_index = lax.axis_index("blk")
    core = shard_index % 2
    core_arr = core.astype(jnp.int32).reshape(1)

    keep, send = pack(core_arr, key_in, value, 0, 1)
    recv = core_swap(send)
    own = [(keep[0], recv[0])]
    pair = [(pair_swap(keep)[0], pair_swap(recv)[0])]
    keep, send = pack(core_arr, key_in, value, 1, chunks)
    recv = core_swap(send)
    own += [(x,) for x in zip_chunks(keep, recv)]
    pair += [(pair_swap(own[c][0]),) for c in range(1, chunks)]
    far = [(relay(pair[0][0], 1), relay(pair[0][1], 1))]
    far += [(relay(pair[c][0], 1),) for c in range(1, chunks)]

    lists = jnp.concatenate([neighbors, counts[:, None]], axis=1)
    lists = jnp.concatenate([lists, core_swap(lists)], axis=0)
    qg_keep, qg_send = pack(core_arr, query, grad_out, 0, chunks)
    qg_recv = core_swap(qg_send)

    home = lists[:, :list_width] // own_blocks
    step = jnp.mod(home // 2 - shard_index // 2 + 1, shard_count // 2)
    pair_step = jnp.where((shard_index // 2) % 2 == 0, 2, 0)
    buf = jnp.where(step == 1, 0, jnp.where(step == pair_step, 1, 2))
    spot = (home % 2) ^ core
    slots = (buf * 2 + spot) * own_blocks + lists[:, :list_width] % own_blocks
    slots = slots.astype(jnp.int32).reshape(-1)
    used = lists[:, list_width]

    kept, crossed, sums = [], [], []
    for c in range(chunks):
        od_keep, to_partner, g_mine, g_pair, g_far = attend(
            c, slots, used, qg_keep, qg_recv, own[c] + pair[c] + far[c], blk
        )
        kept.append(od_keep)
        crossed.append(core_swap(to_partner))
        back = relay(g_far, -1).astype(F32)
        near = pair_swap((g_pair[0] + back[0]).astype(BF16))
        cross = cross_swap((g_pair[1] + back[1]).astype(BF16))
        sums.append((g_mine, near, crossed[c], cross))
    attn_out, grad_query = place(core_arr, kept + crossed, chunks, 0, width)
    head = [x for four in sums[:-1] for x in four]
    grads = place(core_arr, head, chunks - 1, 0, width)
    grad_key, grad_value = place(core_arr, list(sums[-1]), 1, chunks - 1, width, grads)
    return (attn_out, grad_query, grad_key, grad_value)


def solution(mesh):
    spec = P(("groups", "blk"), None)
    flat = P(("groups", "blk"))

    return jax.shard_map(
        local,
        mesh=mesh,
        in_specs=(spec, spec, spec, spec, spec, flat),
        out_specs=(spec, spec, spec, spec),
        check_vma=False,
    )
```

time: 140 us -> 113 us (0.81)
  Pallas kernels: 65.9 us -> 38.5 us
  starting transfers between devices: 26.8 us -> 47.4 us
  local copies, waits for them, and re-layouts: 11.7 us -> 0.51 us
  waiting for transfers between devices: 32.8 us -> 24.4 us
    pallas_call x4, Pallas kernels: 53.8 us -> 31.7 us  [attend(): pl.pallas_call(attend_body, grid=(1,), out_shape=(jax.ShapeDtypeStruct((2...]
    ppermute x21 -> x30, starting transfers between devices: 26.8 us -> 47.4 us  [permuted(): lax.ppermute(x, 'blk', [(i, target(i) % length) for i in range(length)])]
    ppermute x21 -> x30, waiting for transfers between devices: 32.8 us -> 24.4 us  [permuted(): lax.ppermute(x, 'blk', [(i, target(i) % length) for i in range(length)])]
    unnamed x52 -> x4, local copies, waits for them, and re-layouts: 5.97 us -> 0.01 us
    pallas_call x4 -> x6, Pallas kernels: 9.97 us -> 6.67 us  [the longest x3 3.67 us: pack(): pl.pallas_call(functools.partial(pack_body, first), out_shape=(shape, sha...]
    slice x4, local copies, waits for them, and re-layouts: 2.66 us -> 0.14 us  [local(): cross = cross_swap((g_pair[1] + back[1]).astype(BF16))]
    pallas_call x1, Pallas kernels: 2.18 us -> 0.05 us  [zip_chunks(): pl.pallas_call(zip_body, out_shape=(shape,) * keep.shape[0], in_specs=[VM...]
    squeeze x2 -> x0, local copies, waits for them, and re-layouts: 1.61 us -> none  [local(): got[c]]
  transfers between devices with their start and end apart: 21 -> 30, of which waited for: 9 -> 12; matrix products, arithmetic and copies ran while one was open for 5% -> 1% of each run, Pallas kernels for 42% -> 33%
where the time goes in v2:
time: 113 us; the launch traced here: 112 us
  starting transfers between devices  47.4 us (42%)
  Pallas kernels  38.5 us (34%)
  waiting for transfers between devices  24.4 us (22%)
    ppermute x30, starting transfers between devices, permuted(): lax.ppermute(x, 'blk', [(i, target(i) % length) for i in range(length)])  47.4 us
    pallas_call x4, Pallas kernels, attend(): pl.pallas_call(attend_body, grid=(1,), out_shape=(jax.ShapeDtypeStruct((2...  31.7 us
    ppermute x30, waiting for transfers between devices, permuted(): lax.ppermute(x, 'blk', [(i, target(i) % length) for i in range(length)])  24.4 us
    pallas_call x3, Pallas kernels, pack(): pl.pallas_call(functools.partial(pack_body, first), out_shape=(shape, sha...  3.67 us
    pallas_call x3, Pallas kernels, place(): pl.pallas_call(functools.partial(place_body, count, first, len(onto)), ou...  3.01 us
  transfers between devices with their start and end apart: 30, of which 12 were waited for; matrix products, arithmetic and copies ran while one was open for 1% of the time, Pallas kernels for 33%

profile of v2, /device:TPU:1, one launch (start us, length us, event | category | flops | bytes accessed | tf_op | source)
XLA Modules:
  0.0 112.3 jit_solution(5324787605066606019)
XLA Ops:
  0.6 1.0 pack.4
  1.6 0.1 collective-permute-start.2
  1.7 1.3 %pack.5 = (bf16[3,2,256,128]{3,2,1,0:T(8,128)(2,1)S(1)}, bf16[3,2,256,128]{3,2,1,0:T(8,128)(2,1)S(1)}) custom-call(s32[1]{0:T(128)} %bitcast.core_ref, bf16[256,1024]{1,0:T(8,128)(2,1)} %a_ref.5, bf16[256,1024]{1,0:T(8,128)(2,1)} %b_ref.5), custom_call_target="tpu_custom_call" | custom-call | tf_op jit(solution)/shard_map/pack/pallas_call | solution.py:79
  3.0 0.6 collective-permute-start.7
  3.6 1.4 %pack.3 = (bf16[4,2,256,128]{3,2,1,0:T(8,128)(2,1)S(1)}, bf16[4,2,256,128]{3,2,1,0:T(8,128)(2,1)S(1)}) custom-call(s32[1]{0:T(128)} %bitcast.core_ref, bf16[256,1024]{1,0:T(8,128)(2,1)} %a_ref.3, bf16[256,1024]{1,0:T(8,128)(2,1)} %b_ref.3), custom_call_target="tpu_custom_call" | custom-call | tf_op jit(solution)/shard_map/pack/pallas_call | solution.py:79
  5.0 0.1 collective-permute-start.1
  5.1 2.7 %collective-permute-start.3 = (bf16[1,2,256,128]{3,2,1,0:T(8,128)(2,1)S(1)}, bf16[1,2,256,128]{3,2,1,0:T(8,128)(2,1)S(1)}, u32[]{:S(2)}, u32[]{:S(2)}) collective-permute-start(bf16[1,2,256,128]{3,2,1,0:T(8,128)(2,1)S(1)} %get-tuple-element.41), channel_id=1, source_target_pairs={{0,2},{1,3},{2,0},{3,1},{4,6},{5,7},{6,4},{7,5},{8,10},{9,11},{10,... | collective-permute-start | bytes 393224 | tf_op jit(solution)/shard_map/ppermute | solution.py:22
  7.8 0.1 copy.13
  7.9 0.0 collective-permute-done.2
  7.9 0.7 collective-permute-start.4
  8.5 0.1 pad_add_fusion.1
  8.6 0.3 collective-permute-start
  8.9 0.9 collective-permute-done
  9.8 0.1 pad_add_fusion
  9.8 1.7 %collective-permute-done.3 = bf16[1,2,256,128]{3,2,1,0:T(8,128)(2,1)S(1)} collective-permute-done((bf16[1,2,256,128]{3,2,1,0:T(8,128)(2,1)S(1)}, bf16[1,2,256,128]{3,2,1,0:T(8,128)(2,1)S(1)}, u32[]{:S(2)}, u32[]{:S(2)}) %collective-permute-start.3) | collective-permute-done | bytes 131104 | tf_op jit(solution)/shard_map/ppermute | solution.py:22
  11.5 1.2 %collective-permute-start.5 = (bf16[2,256,128]{2,1,0:T(8,128)(2,1)S(1)}, bf16[2,256,128]{2,1,0:T(8,128)(2,1)S(1)}, u32[]{:S(2)}, u32[]{:S(2)}) collective-permute-start(bf16[2,256,128]{2,1,0:T(8,128)(2,1)S(1)} %bitcast.102), channel_id=1, source_target_pairs={{0,4},{1,5},{2,14},{3,15},{4,8},{5,9},{6,2},{7,3},{8,12},{9,13},{1... | collective-permute-start | bytes 393224 | tf_op jit(solution)/shard_map/ppermute | solution.py:22
  12.8 1.6 %collective-permute-done.4 = bf16[1,2,256,128]{3,2,1,0:T(8,128)(2,1)S(1)} collective-permute-done((bf16[1,2,256,128]{3,2,1,0:T(8,128)(2,1)S(1)}, bf16[1,2,256,128]{3,2,1,0:T(8,128)(2,1)S(1)}, u32[]{:S(2)}, u32[]{:S(2)}) %collective-permute-start.4) | collective-permute-done | bytes 131104 | tf_op jit(solution)/shard_map/ppermute | solution.py:22
  14.4 1.2 %collective-permute-start.6 = (bf16[2,256,128]{2,1,0:T(8,128)(2,1)S(1)}, bf16[2,256,128]{2,1,0:T(8,128)(2,1)S(1)}, u32[]{:S(2)}, u32[]{:S(2)}) collective-permute-start(bf16[2,256,128]{2,1,0:T(8,128)(2,1)S(1)} %bitcast.104), channel_id=1, source_target_pairs={{0,4},{1,5},{2,14},{3,15},{4,8},{5,9},{6,2},{7,3},{8,12},{9,13},{1... | collective-permute-start | bytes 393224 | tf_op jit(solution)/shard_map/ppermute | solution.py:22
  15.6 0.1 reshape.92.slots
  15.7 0.0 collective-permute-done.7.recv_ref
  15.7 0.1 zip.1
  15.8 3.3 %collective-permute-start.10 = (bf16[2,2,256,128]{3,2,1,0:T(8,128)(2,1)S(1)}, bf16[2,2,256,128]{3,2,1,0:T(8,128)(2,1)S(1)}, u32[]{:S(2)}, u32[]{:S(2)}) collective-permute-start(bf16[2,2,256,128]{3,2,1,0:T(8,128)(2,1)S(1)} %get-tuple-element.48), channel_id=1, source_target_pairs={{0,2},{1,3},{2,0},{3,1},{4,6},{5,7},{6,4},{7,5},{8,10},{9,11},{10,... | collective-permute-start | bytes 786440 | tf_op jit(solution)/shard_map/ppermute | solution.py:22
  19.1 0.2 slice_reduce_fusion.counts
  19.3 0.1 collective-permute-start.8
  19.4 0.0 collective-permute-done.5
  19.4 1.4 %collective-permute-start.12 = (bf16[2,2,256,128]{3,2,1,0:T(8,128)(2,1)S(1)}, bf16[2,2,256,128]{3,2,1,0:T(8,128)(2,1)S(1)}, u32[]{:S(2)}, u32[]{:S(2)}) collective-permute-start(bf16[2,2,256,128]{3,2,1,0:T(8,128)(2,1)S(1)} %get-tuple-element.50), channel_id=1, source_target_pairs={{0,2},{1,3},{2,0},{3,1},{4,6},{5,7},{6,4},{7,5},{8,10},{9,11},{10,... | collective-permute-start | bytes 786440 | tf_op jit(solution)/shard_map/ppermute | solution.py:22
  20.8 0.3 collective-permute-done.6
  21.1 0.0 collective-permute-done.1.qg_recv
  21.1 7.9 %attend.4 = (bf16[2,256,128]{2,1,0:T(8,128)(2,1)S(1)}, bf16[4,256,128]{2,1,0:T(8,128)(2,1)S(1)}, f32[2,2,128,128]{3,2,1,0:T(8,128)S(1)}, f32[2,2,2,128,128]{4,3,...) custom-call(s32[32]{0:T(128)S(1)} %reshape.92.slots, s32[4]{0:T(128)S(1)} %slice_reduce_fusion.counts, ...), custom_call_target="tpu_custom_call" | custom-call | flops 1610612736 | bytes 2097152 | tf_op jit(solution)/shard_map/attend/pallas_call | solution.py:313
  29.0 1.8 %collective-permute-start.21 = (bf16[2,2,256,128]{3,2,1,0:T(8,128)(2,1)S(1)}, bf16[2,2,256,128]{3,2,1,0:T(8,128)(2,1)S(1)}, u32[]{:S(2)}, u32[]{:S(2)}) collective-permute-start(bf16[2,2,256,128]{3,2,1,0:T(8,128)(2,1)S(1)} %bitcast.99), channel_id=1, source_target_pairs={{0,12},{1,13},{2,6},{3,7},{4,0},{5,1},{6,10},{7,11},{8,4},{9,5},{1... | collective-permute-start | bytes 786440 | tf_op jit(solution)/shard_map/ppermute | solution.py:22
  30.8 0.0 collective-permute-done.10
  30.9 2.7 %collective-permute-start.14 = (bf16[4,256,128]{2,1,0:T(8,128)(2,1)S(1)}, bf16[4,256,128]{2,1,0:T(8,128)(2,1)S(1)}, u32[]{:S(2)}, u32[]{:S(2)}) collective-permute-start(bf16[4,256,128]{2,1,0:T(8,128)(2,1)S(1)} %get-tuple-element.52), channel_id=1, source_target_pairs={{0,1},{1,0},{2,3},{3,2},{4,5},{5,4},{6,7},{7,6},{8,9},{9,8},{10,11... | collective-permute-start | bytes 786440 | tf_op jit(solution)/shard_map/ppermute | solution.py:22
  33.5 0.0 collective-permute-done.8
  33.5 2.3 %collective-permute-done.12 = bf16[2,2,256,128]{3,2,1,0:T(8,128)(2,1)S(1)} collective-permute-done((bf16[2,2,256,128]{3,2,1,0:T(8,128)(2,1)S(1)}, bf16[2,2,256,128]{3,2,1,0:T(8,128)(2,1)S(1)}, u32[]{:S(2)}, u32[]{:S(2)}) %collective-permute-start.12) | collective-permute-done | bytes 262176 | tf_op jit(solution)/shard_map/ppermute | solution.py:22
  35.9 0.1 fusion.9
  35.9 5.2 %collective-permute-done.11 = bf16[2,2,256,128]{3,2,1,0:T(8,128)(2,1)S(1)} collective-permute-done((bf16[2,2,256,128]{3,2,1,0:T(8,128)(2,1)S(1)}, bf16[2,2,256,128]{3,2,1,0:T(8,128)(2,1)S(1)}, u32[]{:S(2)}, u32[]{:S(2)}) %collective-permute-start.11) | collective-permute-done | bytes 262176 | tf_op jit(solution)/shard_map/ppermute | solution.py:22
  41.1 7.9 %attend.6 = (bf16[2,256,128]{2,1,0:T(8,128)(2,1)S(1)}, bf16[4,256,128]{2,1,0:T(8,128)(2,1)S(1)}, f32[2,2,128,128]{3,2,1,0:T(8,128)S(1)}, f32[2,2,2,128,128]{4,3,...) custom-call(s32[32]{0:T(128)S(1)} %reshape.92.slots, s32[4]{0:T(128)S(1)} %slice_reduce_fusion.counts, ...), custom_call_target="tpu_custom_call" | custom-call | flops 1610612736 | bytes 2097152 | tf_op jit(solution)/shard_map/attend/pallas_call | solution.py:313
  49.1 1.8 %collective-permute-start.27 = (bf16[2,2,256,128]{3,2,1,0:T(8,128)(2,1)S(1)}, bf16[2,2,256,128]{3,2,1,0:T(8,128)(2,1)S(1)}, u32[]{:S(2)}, u32[]{:S(2)}) collective-permute-start(bf16[2,2,256,128]{3,2,1,0:T(8,128)(2,1)S(1)} %bitcast.94), channel_id=1, source_target_pairs={{0,12},{1,13},{2,6},{3,7},{4,0},{5,1},{6,10},{7,11},{8,4},{9,5},{1... | collective-permute-start | bytes 786440 | tf_op jit(solution)/shard_map/ppermute | solution.py:22
  50.9 7.9 %attend.5 = (bf16[2,256,128]{2,1,0:T(8,128)(2,1)S(1)}, bf16[4,256,128]{2,1,0:T(8,128)(2,1)S(1)}, f32[2,2,128,128]{3,2,1,0:T(8,128)S(1)}, f32[2,2,2,128,128]{4,3,...) custom-call(s32[32]{0:T(128)S(1)} %reshape.92.slots, s32[4]{0:T(128)S(1)} %slice_reduce_fusion.counts, ...), custom_call_target="tpu_custom_call" | custom-call | flops 1610612736 | bytes 2097152 | tf_op jit(solution)/shard_map/attend/pallas_call | solution.py:313
  58.9 1.0 collective-permute-start.24
  59.9 4.2 %collective-permute-start.16 = (bf16[4,256,128]{2,1,0:T(8,128)(2,1)S(1)}, bf16[4,256,128]{2,1,0:T(8,128)(2,1)S(1)}, u32[]{:S(2)}, u32[]{:S(2)}) collective-permute-start(bf16[4,256,128]{2,1,0:T(8,128)(2,1)S(1)} %get-tuple-element.54), channel_id=1, source_target_pairs={{0,1},{1,0},{2,3},{3,2},{4,5},{5,4},{6,7},{7,6},{8,9},{9,8},{10,11... | collective-permute-start | bytes 786440 | tf_op jit(solution)/shard_map/ppermute | solution.py:22
  64.2 7.9 %attend.7 = (bf16[2,256,128]{2,1,0:T(8,128)(2,1)S(1)}, bf16[4,256,128]{2,1,0:T(8,128)(2,1)S(1)}, f32[2,2,128,128]{3,2,1,0:T(8,128)S(1)}, f32[2,2,2,128,128]{4,3,...) custom-call(s32[32]{0:T(128)S(1)} %reshape.92.slots, s32[4]{0:T(128)S(1)} %slice_reduce_fusion.counts, ...), custom_call_target="tpu_custom_call" | custom-call | flops 1610612736 | bytes 2097152 | tf_op jit(solution)/shard_map/attend/pallas_call | solution.py:313
  72.1 3.0 %collective-permute-start.18 = (bf16[2,2,256,128]{3,2,1,0:T(8,128)(2,1)S(1)}, bf16[2,2,256,128]{3,2,1,0:T(8,128)(2,1)S(1)}, u32[]{:S(2)}, u32[]{:S(2)}) collective-permute-start(bf16[2,2,256,128]{3,2,1,0:T(8,128)(2,1)S(1)} %bitcast.96), channel_id=1, source_target_pairs={{0,12},{1,13},{2,6},{3,7},{4,0},{5,1},{6,10},{7,11},{8,4},{9,5},{1... | collective-permute-start | bytes 786440 | tf_op jit(solution)/shard_map/ppermute | solution.py:22
  75.2 0.3 collective-permute-start.15
  75.6 0.1 fusion.1
  75.6 9.9 %collective-permute-start.22 = (bf16[2,256,128]{2,1,0:T(8,128)(2,1)S(1)}, bf16[2,256,128]{2,1,0:T(8,128)(2,1)S(1)}, u32[]{:S(2)}, u32[]{:S(2)}) collective-permute-start(bf16[2,256,128]{2,1,0:T(8,128)(2,1)S(1)} %get-tuple-element.83), channel_id=1, source_target_pairs={{0,2},{1,3},{2,0},{3,1},{4,6},{5,7},{6,4},{7,5},{8,10},{9,11},{10,... | collective-permute-start | bytes 393224 | tf_op jit(solution)/shard_map/ppermute | solution.py:22
  85.6 0.2 collective-permute-start.23
  85.8 0.5 collective-permute-start.17
  86.2 0.1 fusion.5
  86.4 2.8 %collective-permute-done.22.refs_1_ = bf16[2,256,128]{2,1,0:T(8,128)(2,1)S(1)} collective-permute-done((bf16[2,256,128]{2,1,0:T(8,128)(2,1)S(1)}, bf16[2,256,128]{2,1,0:T(8,128)(2,1)S(1)}, u32[]{:S(2)}, u32[]{:S(2)}) %collective-permute-start.22) | collective-permute-done | bytes 131104 | tf_op jit(solution)/shard_map/ppermute | solution.py:22
  89.2 4.3 %collective-permute-start.28 = (bf16[2,256,128]{2,1,0:T(8,128)(2,1)S(1)}, bf16[2,256,128]{2,1,0:T(8,128)(2,1)S(1)}, u32[]{:S(2)}, u32[]{:S(2)}) collective-permute-start(bf16[2,256,128]{2,1,0:T(8,128)(2,1)S(1)} %get-tuple-element.75), channel_id=1, source_target_pairs={{0,2},{1,3},{2,0},{3,1},{4,6},{5,7},{6,4},{7,5},{8,10},{9,11},{10,... | collective-permute-start | bytes 393224 | tf_op jit(solution)/shard_map/ppermute | solution.py:22
  93.5 1.6 %collective-permute-start.25 = (bf16[2,256,128]{2,1,0:T(8,128)(2,1)S(1)}, bf16[2,256,128]{2,1,0:T(8,128)(2,1)S(1)}, u32[]{:S(2)}, u32[]{:S(2)}) collective-permute-start(bf16[2,256,128]{2,1,0:T(8,128)(2,1)S(1)} %get-tuple-element.79), channel_id=1, source_target_pairs={{0,2},{1,3},{2,0},{3,1},{4,6},{5,7},{6,4},{7,5},{8,10},{9,11},{10,... | collective-permute-start | bytes 393224 | tf_op jit(solution)/shard_map/ppermute | solution.py:22
  95.1 0.5 collective-permute-start.26
  95.6 0.1 fusion.13
  95.7 1.4 %collective-permute-start.19 = (bf16[2,256,128]{2,1,0:T(8,128)(2,1)S(1)}, bf16[2,256,128]{2,1,0:T(8,128)(2,1)S(1)}, u32[]{:S(2)}, u32[]{:S(2)}) collective-permute-start(bf16[2,256,128]{2,1,0:T(8,128)(2,1)S(1)} %get-tuple-element.87), channel_id=1, source_target_pairs={{0,2},{1,3},{2,0},{3,1},{4,6},{5,7},{6,4},{7,5},{8,10},{9,11},{10,... | collective-permute-start | bytes 393224 | tf_op jit(solution)/shard_map/ppermute | solution.py:22
  97.1 0.2 collective-permute-done.28.refs_9_
  97.3 2.4 %collective-permute-start.20 = (bf16[2,256,128]{2,1,0:T(8,128)(2,1)S(1)}, bf16[2,256,128]{2,1,0:T(8,128)(2,1)S(1)}, u32[]{:S(2)}, u32[]{:S(2)}) collective-permute-start(bf16[2,256,128]{2,1,0:T(8,128)(2,1)S(1)} %get-tuple-element.86), channel_id=1, source_target_pairs={{0,3},{1,2},{2,1},{3,0},{4,7},{5,6},{6,5},{7,4},{8,11},{9,10},{10,... | collective-permute-start | bytes 393224 | tf_op jit(solution)/shard_map/ppermute | solution.py:22
  99.7 1.1 place.3
  100.8 2.1 %collective-permute-done.25.refs_5_ = bf16[2,256,128]{2,1,0:T(8,128)(2,1)S(1)} collective-permute-done((bf16[2,256,128]{2,1,0:T(8,128)(2,1)S(1)}, bf16[2,256,128]{2,1,0:T(8,128)(2,1)S(1)}, u32[]{:S(2)}, u32[]{:S(2)}) %collective-permute-start.25) | collective-permute-done | bytes 131104 | tf_op jit(solution)/shard_map/ppermute | solution.py:22
  102.9 2.9 %collective-permute-done.26.refs_7_ = bf16[2,256,128]{2,1,0:T(8,128)(2,1)S(1)} collective-permute-done((bf16[2,256,128]{2,1,0:T(8,128)(2,1)S(1)}, bf16[2,256,128]{2,1,0:T(8,128)(2,1)S(1)}, u32[]{:S(2)}, u32[]{:S(2)}) %collective-permute-start.26) | collective-permute-done | bytes 131104 | tf_op jit(solution)/shard_map/ppermute | solution.py:22
  105.8 1.1 %place.4 = (bf16[256,1024]{1,0:T(8,128)(2,1)}, bf16[256,1024]{1,0:T(8,128)(2,1)}) custom-call(s32[1]{0:T(128)} %bitcast.core_ref, f32[2,256,128]{2,1,0:T(8,128)S(1)} %bitcast.83, bf16[2,256,128]{2,1,0:T(8,128)(2,1)S(1)} %collective-permute-done.22.refs_1_, bf16[4,256,128]{2,1,0:T(8,128)(2,1)S(1)} %collective-permute-done.14.refs_4_.refs_2_, ...), custom_call_target="tpu_custom_call" | custom-call | tf_op jit(solution)/shard_map/place/pallas_call | solution.py:135
  107.0 1.6 %collective-permute-done.19.refs_1_ = bf16[2,256,128]{2,1,0:T(8,128)(2,1)S(1)} collective-permute-done((bf16[2,256,128]{2,1,0:T(8,128)(2,1)S(1)}, bf16[2,256,128]{2,1,0:T(8,128)(2,1)S(1)}, u32[]{:S(2)}, u32[]{:S(2)}) %collective-permute-start.19) | collective-permute-done | bytes 131104 | tf_op jit(solution)/shard_map/ppermute | solution.py:22
  108.6 2.8 %collective-permute-done.20.refs_3_ = bf16[2,256,128]{2,1,0:T(8,128)(2,1)S(1)} collective-permute-done((bf16[2,256,128]{2,1,0:T(8,128)(2,1)S(1)}, bf16[2,256,128]{2,1,0:T(8,128)(2,1)S(1)}, u32[]{:S(2)}, u32[]{:S(2)}) %collective-permute-start.20) | collective-permute-done | bytes 131104 | tf_op jit(solution)/shard_map/ppermute | solution.py:22
  111.4 0.8 place.5
  (29 shorter events, 0.4 us)
Async XLA Ops:
  1.6 6.2 %collective-permute-start.2 = (bf16[1,2,256,128]{3,2,1,0:T(8,128)(2,1)S(1)}, bf16[1,2,256,128]{3,2,1,0:T(8,128)(2,1)S(1)}, u32[]{:S(2)}, u32[]{:S(2)}) collective-permute-start(bf16[1,2,256,128]{3,2,1,0:T(8,128)(2,1)S(1)} %get-tuple-element.42), channel_id=1, source_target_pairs={{0,1},{1,0},{2,3},{3,2},{4,5},{5,4},{6,7},{7,6},{8,9},{9,8},{10,11... | collective-permute-start | bytes 393224 | tf_op jit(solution)/shard_map/ppermute | solution.py:22
  3.0 12.7 %collective-permute-start.7 = (bf16[3,2,256,128]{3,2,1,0:T(8,128)(2,1)S(1)}, bf16[3,2,256,128]{3,2,1,0:T(8,128)(2,1)S(1)}, u32[]{:S(2)}, u32[]{:S(2)}) collective-permute-start(bf16[3,2,256,128]{3,2,1,0:T(8,128)(2,1)S(1)} %get-tuple-element.45), channel_id=1, source_target_pairs={{0,1},{1,0},{2,3},{3,2},{4,5},{5,4},{6,7},{7,6},{8,9},{9,8},{10,11... | collective-permute-start | bytes 1179656 | tf_op jit(solution)/shard_map/ppermute | solution.py:22
  5.0 16.1 %collective-permute-start.1 = (bf16[4,2,256,128]{3,2,1,0:T(8,128)(2,1)S(1)}, bf16[4,2,256,128]{3,2,1,0:T(8,128)(2,1)S(1)}, u32[]{:S(2)}, u32[]{:S(2)}) collective-permute-start(bf16[4,2,256,128]{3,2,1,0:T(8,128)(2,1)S(1)} %get-tuple-element.40), channel_id=1, source_target_pairs={{0,1},{1,0},{2,3},{3,2},{4,5},{5,4},{6,7},{7,6},{8,9},{9,8},{10,11... | collective-permute-start | bytes 1572872 | tf_op jit(solution)/shard_map/ppermute | solution.py:22
  5.1 2.7 %copy-start.1 = (s32[2]{0:T(128)S(1)}, s32[2]{0:T(128)}, u32[]{:S(2)}) copy-start(s32[2]{0:T(128)} %param.11) | copy-start | bytes 28
  5.1 6.5 %collective-permute-start.3 = (bf16[1,2,256,128]{3,2,1,0:T(8,128)(2,1)S(1)}, bf16[1,2,256,128]{3,2,1,0:T(8,128)(2,1)S(1)}, u32[]{:S(2)}, u32[]{:S(2)}) collective-permute-start(bf16[1,2,256,128]{3,2,1,0:T(8,128)(2,1)S(1)} %get-tuple-element.41), channel_id=1, source_target_pairs={{0,2},{1,3},{2,0},{3,1},{4,6},{5,7},{6,4},{7,5},{8,10},{9,11},{10,... | collective-permute-start | bytes 393224 | tf_op jit(solution)/shard_map/ppermute | solution.py:22
  7.8 0.8 copy-start
  7.9 6.5 %collective-permute-start.4 = (bf16[1,2,256,128]{3,2,1,0:T(8,128)(2,1)S(1)}, bf16[1,2,256,128]{3,2,1,0:T(8,128)(2,1)S(1)}, u32[]{:S(2)}, u32[]{:S(2)}) collective-permute-start(bf16[1,2,256,128]{3,2,1,0:T(8,128)(2,1)S(1)} %collective-permute-done.2), channel_id=1, source_target_pairs={{0,2},{1,3},{2,0},{3,1},{4,6},{5,7},{6,4},{7,5},{8,10},{9,11},{10,... | collective-permute-start | bytes 393224 | tf_op jit(solution)/shard_map/ppermute | solution.py:22
  8.6 1.2 %collective-permute-start = (s32[2,9]{1,0:T(2,128)S(1)}, s32[2,9]{1,0:T(2,128)S(1)}, u32[]{:S(2)}, u32[]{:S(2)}) collective-permute-start(s32[2,9]{1,0:T(2,128)S(1)} %pad_add_fusion.1), channel_id=1, source_target_pairs={{0,1},{1,0},{2,3},{3,2},{4,5},{5,4},{6,7},{7,6},{8,9},{9,8},{10,11... | collective-permute-start | bytes 224 | tf_op jit(solution)/shard_map/ppermute | solution.py:22
  11.5 7.8 %collective-permute-start.5 = (bf16[2,256,128]{2,1,0:T(8,128)(2,1)S(1)}, bf16[2,256,128]{2,1,0:T(8,128)(2,1)S(1)}, u32[]{:S(2)}, u32[]{:S(2)}) collective-permute-start(bf16[2,256,128]{2,1,0:T(8,128)(2,1)S(1)} %bitcast.102), channel_id=1, source_target_pairs={{0,4},{1,5},{2,14},{3,15},{4,8},{5,9},{6,2},{7,3},{8,12},{9,13},{1... | collective-permute-start | bytes 393224 | tf_op jit(solution)/shard_map/ppermute | solution.py:22
  14.4 6.7 %collective-permute-start.6 = (bf16[2,256,128]{2,1,0:T(8,128)(2,1)S(1)}, bf16[2,256,128]{2,1,0:T(8,128)(2,1)S(1)}, u32[]{:S(2)}, u32[]{:S(2)}) collective-permute-start(bf16[2,256,128]{2,1,0:T(8,128)(2,1)S(1)} %bitcast.104), channel_id=1, source_target_pairs={{0,4},{1,5},{2,14},{3,15},{4,8},{5,9},{6,2},{7,3},{8,12},{9,13},{1... | collective-permute-start | bytes 393224 | tf_op jit(solution)/shard_map/ppermute | solution.py:22
  15.8 15.0 %collective-permute-start.10 = (bf16[2,2,256,128]{3,2,1,0:T(8,128)(2,1)S(1)}, bf16[2,2,256,128]{3,2,1,0:T(8,128)(2,1)S(1)}, u32[]{:S(2)}, u32[]{:S(2)}) collective-permute-start(bf16[2,2,256,128]{3,2,1,0:T(8,128)(2,1)S(1)} %get-tuple-element.48), channel_id=1, source_target_pairs={{0,2},{1,3},{2,0},{3,1},{4,6},{5,7},{6,4},{7,5},{8,10},{9,11},{10,... | collective-permute-start | bytes 786440 | tf_op jit(solution)/shard_map/ppermute | solution.py:22
  19.3 14.2 %collective-permute-start.8 = (bf16[2,2,256,128]{3,2,1,0:T(8,128)(2,1)S(1)}, bf16[2,2,256,128]{3,2,1,0:T(8,128)(2,1)S(1)}, u32[]{:S(2)}, u32[]{:S(2)}) collective-permute-start(bf16[2,2,256,128]{3,2,1,0:T(8,128)(2,1)S(1)} %get-tuple-element.46), channel_id=1, source_target_pairs={{0,2},{1,3},{2,0},{3,1},{4,6},{5,7},{6,4},{7,5},{8,10},{9,11},{10,... | collective-permute-start | bytes 786440 | tf_op jit(solution)/shard_map/ppermute | solution.py:22
  19.4 16.4 %collective-permute-start.12 = (bf16[2,2,256,128]{3,2,1,0:T(8,128)(2,1)S(1)}, bf16[2,2,256,128]{3,2,1,0:T(8,128)(2,1)S(1)}, u32[]{:S(2)}, u32[]{:S(2)}) collective-permute-start(bf16[2,2,256,128]{3,2,1,0:T(8,128)(2,1)S(1)} %get-tuple-element.50), channel_id=1, source_target_pairs={{0,2},{1,3},{2,0},{3,1},{4,6},{5,7},{6,4},{7,5},{8,10},{9,11},{10,... | collective-permute-start | bytes 786440 | tf_op jit(solution)/shard_map/ppermute | solution.py:22
  29.0 6.8 %collective-permute-start.21 = (bf16[2,2,256,128]{3,2,1,0:T(8,128)(2,1)S(1)}, bf16[2,2,256,128]{3,2,1,0:T(8,128)(2,1)S(1)}, u32[]{:S(2)}, u32[]{:S(2)}) collective-permute-start(bf16[2,2,256,128]{3,2,1,0:T(8,128)(2,1)S(1)} %bitcast.99), channel_id=1, source_target_pairs={{0,12},{1,13},{2,6},{3,7},{4,0},{5,1},{6,10},{7,11},{8,4},{9,5},{1... | collective-permute-start | bytes 786440 | tf_op jit(solution)/shard_map/ppermute | solution.py:22
  30.8 10.3 %collective-permute-start.11 = (bf16[2,2,256,128]{3,2,1,0:T(8,128)(2,1)S(1)}, bf16[2,2,256,128]{3,2,1,0:T(8,128)(2,1)S(1)}, u32[]{:S(2)}, u32[]{:S(2)}) collective-permute-start(bf16[2,2,256,128]{3,2,1,0:T(8,128)(2,1)S(1)} %collective-permute-done.10), channel_id=1, source_target_pairs={{0,4},{1,5},{2,14},{3,15},{4,8},{5,9},{6,2},{7,3},{8,12},{9,13},{1... | collective-permute-start | bytes 786440 | tf_op jit(solution)/shard_map/ppermute | solution.py:22
  30.9 54.7 %collective-permute-start.14 = (bf16[4,256,128]{2,1,0:T(8,128)(2,1)S(1)}, bf16[4,256,128]{2,1,0:T(8,128)(2,1)S(1)}, u32[]{:S(2)}, u32[]{:S(2)}) collective-permute-start(bf16[4,256,128]{2,1,0:T(8,128)(2,1)S(1)} %get-tuple-element.52), channel_id=1, source_target_pairs={{0,1},{1,0},{2,3},{3,2},{4,5},{5,4},{6,7},{7,6},{8,9},{9,8},{10,11... | collective-permute-start | bytes 786440 | tf_op jit(solution)/shard_map/ppermute | solution.py:22
  33.5 17.4 %collective-permute-start.9 = (bf16[2,2,256,128]{3,2,1,0:T(8,128)(2,1)S(1)}, bf16[2,2,256,128]{3,2,1,0:T(8,128)(2,1)S(1)}, u32[]{:S(2)}, u32[]{:S(2)}) collective-permute-start(bf16[2,2,256,128]{3,2,1,0:T(8,128)(2,1)S(1)} %collective-permute-done.8), channel_id=1, source_target_pairs={{0,4},{1,5},{2,14},{3,15},{4,8},{5,9},{6,2},{7,3},{8,12},{9,13},{1... | collective-permute-start | bytes 786440 | tf_op jit(solution)/shard_map/ppermute | solution.py:22
  35.8 28.3 %collective-permute-start.13 = (bf16[2,2,256,128]{3,2,1,0:T(8,128)(2,1)S(1)}, bf16[2,2,256,128]{3,2,1,0:T(8,128)(2,1)S(1)}, u32[]{:S(2)}, u32[]{:S(2)}) collective-permute-start(bf16[2,2,256,128]{3,2,1,0:T(8,128)(2,1)S(1)} %collective-permute-done.12), channel_id=1, source_target_pairs={{0,4},{1,5},{2,14},{3,15},{4,8},{5,9},{6,2},{7,3},{8,12},{9,13},{1... | collective-permute-start | bytes 786440 | tf_op jit(solution)/shard_map/ppermute | solution.py:22
  49.1 26.1 %collective-permute-start.27 = (bf16[2,2,256,128]{3,2,1,0:T(8,128)(2,1)S(1)}, bf16[2,2,256,128]{3,2,1,0:T(8,128)(2,1)S(1)}, u32[]{:S(2)}, u32[]{:S(2)}) collective-permute-start(bf16[2,2,256,128]{3,2,1,0:T(8,128)(2,1)S(1)} %bitcast.94), channel_id=1, source_target_pairs={{0,12},{1,13},{2,6},{3,7},{4,0},{5,1},{6,10},{7,11},{8,4},{9,5},{1... | collective-permute-start | bytes 786440 | tf_op jit(solution)/shard_map/ppermute | solution.py:22
  58.9 16.8 %collective-permute-start.24 = (bf16[2,2,256,128]{3,2,1,0:T(8,128)(2,1)S(1)}, bf16[2,2,256,128]{3,2,1,0:T(8,128)(2,1)S(1)}, u32[]{:S(2)}, u32[]{:S(2)}) collective-permute-start(bf16[2,2,256,128]{3,2,1,0:T(8,128)(2,1)S(1)} %bitcast.95), channel_id=1, source_target_pairs={{0,12},{1,13},{2,6},{3,7},{4,0},{5,1},{6,10},{7,11},{8,4},{9,5},{1... | collective-permute-start | bytes 786440 | tf_op jit(solution)/shard_map/ppermute | solution.py:22
  59.9 33.6 %collective-permute-start.16 = (bf16[4,256,128]{2,1,0:T(8,128)(2,1)S(1)}, bf16[4,256,128]{2,1,0:T(8,128)(2,1)S(1)}, u32[]{:S(2)}, u32[]{:S(2)}) collective-permute-start(bf16[4,256,128]{2,1,0:T(8,128)(2,1)S(1)} %get-tuple-element.54), channel_id=1, source_target_pairs={{0,1},{1,0},{2,3},{3,2},{4,5},{5,4},{6,7},{7,6},{8,9},{9,8},{10,11... | collective-permute-start | bytes 786440 | tf_op jit(solution)/shard_map/ppermute | solution.py:22
  72.1 13.7 %collective-permute-start.18 = (bf16[2,2,256,128]{3,2,1,0:T(8,128)(2,1)S(1)}, bf16[2,2,256,128]{3,2,1,0:T(8,128)(2,1)S(1)}, u32[]{:S(2)}, u32[]{:S(2)}) collective-permute-start(bf16[2,2,256,128]{3,2,1,0:T(8,128)(2,1)S(1)} %bitcast.96), channel_id=1, source_target_pairs={{0,12},{1,13},{2,6},{3,7},{4,0},{5,1},{6,10},{7,11},{8,4},{9,5},{1... | collective-permute-start | bytes 786440 | tf_op jit(solution)/shard_map/ppermute | solution.py:22
  75.2 19.9 %collective-permute-start.15 = (bf16[4,256,128]{2,1,0:T(8,128)(2,1)S(1)}, bf16[4,256,128]{2,1,0:T(8,128)(2,1)S(1)}, u32[]{:S(2)}, u32[]{:S(2)}) collective-permute-start(bf16[4,256,128]{2,1,0:T(8,128)(2,1)S(1)} %get-tuple-element.53), channel_id=1, source_target_pairs={{0,1},{1,0},{2,3},{3,2},{4,5},{5,4},{6,7},{7,6},{8,9},{9,8},{10,11... | collective-permute-start | bytes 786440 | tf_op jit(solution)/shard_map/ppermute | solution.py:22
  75.6 13.5 %collective-permute-start.22 = (bf16[2,256,128]{2,1,0:T(8,128)(2,1)S(1)}, bf16[2,256,128]{2,1,0:T(8,128)(2,1)S(1)}, u32[]{:S(2)}, u32[]{:S(2)}) collective-permute-start(bf16[2,256,128]{2,1,0:T(8,128)(2,1)S(1)} %get-tuple-element.83), channel_id=1, source_target_pairs={{0,2},{1,3},{2,0},{3,1},{4,6},{5,7},{6,4},{7,5},{8,10},{9,11},{10,... | collective-permute-start | bytes 393224 | tf_op jit(solution)/shard_map/ppermute | solution.py:22
  85.6 7.9 %collective-permute-start.23 = (bf16[2,256,128]{2,1,0:T(8,128)(2,1)S(1)}, bf16[2,256,128]{2,1,0:T(8,128)(2,1)S(1)}, u32[]{:S(2)}, u32[]{:S(2)}) collective-permute-start(bf16[2,256,128]{2,1,0:T(8,128)(2,1)S(1)} %get-tuple-element.82), channel_id=1, source_target_pairs={{0,3},{1,2},{2,1},{3,0},{4,7},{5,6},{6,5},{7,4},{8,11},{9,10},{10,... | collective-permute-start | bytes 393224 | tf_op jit(solution)/shard_map/ppermute | solution.py:22
  85.8 9.9 %collective-permute-start.17 = (bf16[4,256,128]{2,1,0:T(8,128)(2,1)S(1)}, bf16[4,256,128]{2,1,0:T(8,128)(2,1)S(1)}, u32[]{:S(2)}, u32[]{:S(2)}) collective-permute-start(bf16[4,256,128]{2,1,0:T(8,128)(2,1)S(1)} %get-tuple-element.55), channel_id=1, source_target_pairs={{0,1},{1,0},{2,3},{3,2},{4,5},{5,4},{6,7},{7,6},{8,9},{9,8},{10,11... | collective-permute-start | bytes 786440 | tf_op jit(solution)/shard_map/ppermute | solution.py:22
  89.2 8.2 %collective-permute-start.28 = (bf16[2,256,128]{2,1,0:T(8,128)(2,1)S(1)}, bf16[2,256,128]{2,1,0:T(8,128)(2,1)S(1)}, u32[]{:S(2)}, u32[]{:S(2)}) collective-permute-start(bf16[2,256,128]{2,1,0:T(8,128)(2,1)S(1)} %get-tuple-element.75), channel_id=1, source_target_pairs={{0,2},{1,3},{2,0},{3,1},{4,6},{5,7},{6,4},{7,5},{8,10},{9,11},{10,... | collective-permute-start | bytes 393224 | tf_op jit(solution)/shard_map/ppermute | solution.py:22
  93.5 7.4 %collective-permute-start.29 = (bf16[2,256,128]{2,1,0:T(8,128)(2,1)S(1)}, bf16[2,256,128]{2,1,0:T(8,128)(2,1)S(1)}, u32[]{:S(2)}, u32[]{:S(2)}) collective-permute-start(bf16[2,256,128]{2,1,0:T(8,128)(2,1)S(1)} %get-tuple-element.74), channel_id=1, source_target_pairs={{0,3},{1,2},{2,1},{3,0},{4,7},{5,6},{6,5},{7,4},{8,11},{9,10},{10,... | collective-permute-start | bytes 393224 | tf_op jit(solution)/shard_map/ppermute | solution.py:22
  93.5 9.5 %collective-permute-start.25 = (bf16[2,256,128]{2,1,0:T(8,128)(2,1)S(1)}, bf16[2,256,128]{2,1,0:T(8,128)(2,1)S(1)}, u32[]{:S(2)}, u32[]{:S(2)}) collective-permute-start(bf16[2,256,128]{2,1,0:T(8,128)(2,1)S(1)} %get-tuple-element.79), channel_id=1, source_target_pairs={{0,2},{1,3},{2,0},{3,1},{4,6},{5,7},{6,4},{7,5},{8,10},{9,11},{10,... | collective-permute-start | bytes 393224 | tf_op jit(solution)/shard_map/ppermute | solution.py:22
  95.1 10.7 %collective-permute-start.26 = (bf16[2,256,128]{2,1,0:T(8,128)(2,1)S(1)}, bf16[2,256,128]{2,1,0:T(8,128)(2,1)S(1)}, u32[]{:S(2)}, u32[]{:S(2)}) collective-permute-start(bf16[2,256,128]{2,1,0:T(8,128)(2,1)S(1)} %get-tuple-element.78), channel_id=1, source_target_pairs={{0,3},{1,2},{2,1},{3,0},{4,7},{5,6},{6,5},{7,4},{8,11},{9,10},{10,... | collective-permute-start | bytes 393224 | tf_op jit(solution)/shard_map/ppermute | solution.py:22
  95.7 12.9 %collective-permute-start.19 = (bf16[2,256,128]{2,1,0:T(8,128)(2,1)S(1)}, bf16[2,256,128]{2,1,0:T(8,128)(2,1)S(1)}, u32[]{:S(2)}, u32[]{:S(2)}) collective-permute-start(bf16[2,256,128]{2,1,0:T(8,128)(2,1)S(1)} %get-tuple-element.87), channel_id=1, source_target_pairs={{0,2},{1,3},{2,0},{3,1},{4,6},{5,7},{6,4},{7,5},{8,10},{9,11},{10,... | collective-permute-start | bytes 393224 | tf_op jit(solution)/shard_map/ppermute | solution.py:22
  97.3 14.0 %collective-permute-start.20 = (bf16[2,256,128]{2,1,0:T(8,128)(2,1)S(1)}, bf16[2,256,128]{2,1,0:T(8,128)(2,1)S(1)}, u32[]{:S(2)}, u32[]{:S(2)}) collective-permute-start(bf16[2,256,128]{2,1,0:T(8,128)(2,1)S(1)} %get-tuple-element.86), channel_id=1, source_target_pairs={{0,3},{1,2},{2,1},{3,0},{4,7},{5,6},{6,5},{7,4},{8,11},{9,10},{10,... | collective-permute-start | bytes 393224 | tf_op jit(solution)/shard_map/ppermute | solution.py:22
